TPU v7x, 32 devices: a whole 2x2x4 slice. The times are simulated.
32 devices in a mesh: gx: 4 (over z), gy: 8 (over y, x, core).
Axes of the slice: x: 2, y: 2, z: 4, core: 2. Of those that a mesh axis runs over, the one named last changes fastest.
Arguments:
- outer_state: bfloat16 [5, 64, 16, 8192], P(None, None, 'gy', 'gx'), may hold values from -6 to 6
- derivative: bfloat16 [3, 64, 64], replicated, may hold values from -0.75 to 0.75
- stiffness: float32 [64, 64], replicated, may hold values from -0.75 to 0.75
- wall_rhs: float32 [1024, 320], P(('gx', 'gy')), may hold values from -6 to 6
- wall_sigma: float32 [1024, 320], P(('gx', 'gy')), may hold values from 0.2 to 5
- wall_inverse: bfloat16 [1024, 320, 320], P(('gx', 'gy')), as said below
- wall_count: int32 [4, 8], P('gx', 'gy'), may hold values from 1 to 32, as said below
Outputs:
- outer_residual: bfloat16 [5, 64, 16, 8192], P(None, None, 'gy', 'gx')
- wall_update: float32 [1024, 320], P(('gx', 'gy'))
Inputs may be any that keep to these rules, and one draw needn't show every extreme that they name: `wall_count`: live near-wall elements fill the first slots of a device; every device with gy index 0 holds 32, every other at most 8. `wall_inverse`: every block is invertible.
All inputs are finite; a program needn't handle non-finite values.
Results may differ from a plain program's by a relative error of at most 0.0045.
Values may be sent and summed in bfloat16 or wider, within the bound.
No kernel may reach another device: no remote copies, remote signals or barrier semaphores. Data moves between devices by JAX's collectives and lax.ppermute only.
A program may use at most 128 MiB of HBM per device.

v0:
```python
import jax
import jax.numpy as jnp
from jax import lax
from jax.sharding import PartitionSpec as P

Q = 4
ITERS = 3


time_step = 0.3
coupling = 0.25
upwind_x = 2.0
upwind_y = 1.0
advection = (1.0, 0.5, 0.25)
group_size = 4


def passed_along(array, axis, by):
    count = lax.axis_size(axis)
    return lax.ppermute(array, axis, [(i, (i + by) % count) for i in range(count)])


def from_behind(array, axis, by):
    count = lax.axis_size(axis)
    pairs = [(i, i + by) for i in range(count) if 0 <= i + by < count]
    return lax.ppermute(array, axis, pairs)


def for_sending(array):
    return jax.tree.map(lambda a: a.astype(jnp.bfloat16) if a.dtype == jnp.float32 else a, array)


def padded(array, sides, width):
    for axis, dim in sides:
        count, length = (lax.axis_size(axis), array.shape[dim])
        up = [(i, (i + 1) % count) for i in range(count)]
        down = [(j, i) for i, j in up]
        last = lax.slice_in_dim(array, length - width, length, axis=dim)
        initial = lax.slice_in_dim(array, 0, width, axis=dim)
        before = lax.ppermute(last, axis, up)
        after = lax.ppermute(initial, axis, down)
        array = jnp.concatenate([before, array, after], axis=dim)
    return array


def least_squares(hess, beta):
    gram = jnp.dot(hess.T, hess, precision=lax.Precision.HIGHEST)
    target = beta * hess[0]
    lower = jnp.linalg.cholesky(gram)
    middle = lax.linalg.triangular_solve(lower, target[:, None], left_side=True, lower=True)
    return lax.linalg.triangular_solve(lower, middle, left_side=True, lower=True, transpose_a=True)[
        :, 0
    ]


def explicit_residual(outer_state, derivative):
    comps, nodes, rows, cols = outer_state.shape
    state = outer_state.astype(jnp.float32)
    fluxes = jnp.stack([state * (advection[d] + state[1 + d]) for d in range(3)]).astype(
        jnp.bfloat16
    )
    volume = jnp.einsum("dmn,dvnyx->vmyx", derivative, fluxes, preferred_element_type=jnp.float32)
    cube = outer_state.reshape(comps, Q, Q, Q, rows, cols)
    last_column = cube[:, :, :, Q - 1, :, cols - 1]
    came_x = passed_along(last_column, "gx", 1)
    upstream_x = jnp.concatenate([came_x[..., None], cube[:, :, :, Q - 1, :, :-1]], axis=-1)
    jump_x = upstream_x.astype(jnp.float32) - cube[:, :, :, 0].astype(jnp.float32)
    top_row = cube[:, :, Q - 1, :, rows - 1, :]
    came_y = from_behind(top_row, "gy", 1)
    upstream_y = jnp.concatenate([came_y[:, :, :, None, :], cube[:, :, Q - 1, :, :-1, :]], axis=3)
    jump_y = upstream_y.astype(jnp.float32) - cube[:, :, 0].astype(jnp.float32)
    resid = volume.reshape(comps, Q, Q, Q, rows, cols)
    resid = resid.at[:, :, :, 0].add(upwind_x * jump_x)
    resid = resid.at[:, :, 0].add(upwind_y * jump_y)
    return resid.reshape(comps, nodes, rows, cols)


def apply_blocks(blocks, vectors, groups):

    def one_group(group, result):
        start = group * group_size
        block = lax.dynamic_slice_in_dim(blocks, start, group_size, 0).astype(jnp.float32)
        piece = lax.dynamic_slice_in_dim(vectors, start, group_size, 0)
        product = jnp.einsum("gij,gj->gi", block, piece, precision=lax.Precision.HIGHEST)
        return lax.dynamic_update_slice_in_dim(result, product, start, 0)

    return lax.fori_loop(0, groups, one_group, jnp.zeros_like(vectors))


def per_device(outer_state, derivative, stiffness, wall_rhs, wall_sigma, wall_inverse, wall_count):
    resid = explicit_residual(outer_state, derivative)
    outer_residual = resid.astype(jnp.bfloat16)
    slots_dev, order_size = wall_rhs.shape
    comps = outer_state.shape[0]
    nodes = outer_state.shape[1]
    count = wall_count[0, 0]
    slots = jnp.arange(slots_dev, dtype=jnp.int32)
    live = (slots < count).astype(jnp.float32)
    trace = resid[:, :, 0, :slots_dev].transpose(2, 0, 1).reshape(slots_dev, order_size)
    own_groups = (count + group_size - 1) // group_size
    rhs = live[:, None] * (wall_rhs + time_step * trace)
    beta = jnp.sqrt(lax.psum(jnp.sum(rhs * rhs), ("gx", "gy")))
    basis = [rhs / beta]
    directions = []
    columns = []
    for column_index in range(ITERS):
        direction = apply_blocks(wall_inverse, basis[column_index], own_groups)
        directions.append(direction)
        stiff = jnp.einsum(
            "wvn,nm->wvm",
            direction.reshape(slots_dev, comps, nodes),
            stiffness,
            precision=lax.Precision.HIGHEST,
        ).reshape(slots_dev, order_size)
        beside_all = padded(for_sending(direction[None]), (("gx", 0),), 1)
        image = live[:, None] * (
            direction
            + time_step * (wall_sigma * direction + stiff)
            - coupling * (beside_all[0] + beside_all[2])
        )
        entries = []
        for row_index in range(column_index + 1):
            value = lax.psum(jnp.sum(image * basis[row_index]), ("gx", "gy"))
            image = image - value * basis[row_index]
            entries.append(value)
        length = jnp.sqrt(lax.psum(jnp.sum(image * image), ("gx", "gy")))
        entries.append(length)
        basis.append(image / length)
        columns.append(
            jnp.concatenate(
                [jnp.stack(entries), jnp.zeros((ITERS - column_index - 1,), jnp.float32)]
            )
        )
    hess = jnp.stack(columns, axis=1)
    weights = least_squares(hess, beta)
    wall_update = jnp.zeros((slots_dev, order_size), jnp.float32)
    for column_index in range(ITERS):
        wall_update = wall_update + weights[column_index] * directions[column_index]
    return (outer_residual, wall_update)


def solution(mesh):
    in_specs = (
        P(None, None, "gy", "gx"),
        P(),
        P(),
        P(("gx", "gy"), None),
        P(("gx", "gy"), None),
        P(("gx", "gy"), None, None),
        P("gx", "gy"),
    )
    out_specs = (P(None, None, "gy", "gx"), P(("gx", "gy"), None))
    return jax.shard_map(
        per_device, mesh=mesh, in_specs=in_specs, out_specs=out_specs, check_vma=False
    )
```

profile of v0, /device:TPU:0, one launch (start us, length us, event | category | flops | bytes accessed | tf_op | source)
XLA Modules:
  0.0 582.9 jit_solution(2800993213544158704)
XLA Ops:
  2.0 3.1 collective-permute-start
  5.1 3.7 fusion.53
  9.8 2.2 collective-permute-start.1
  12.0 3.5 copy_convert_fusion
  15.5 1.6 slice.152
  19.9 2.2 fusion.29
  22.1 3.1 fusion.21
  25.3 3.4 fusion.18
  28.6 7.2 %reshape.210 = f32[5,4,4,4,2,2048]{5,3,2,1,4,0:T(4,128)} reshape(f32[5,64,2,2048]{3,1,2,0:T(8,128)} %fusion.18) | data formatting | bytes 10485760 | tf_op jit(solution)/shard_map/reshape | solution.py:72
  35.9 1.5 copy.75
  38.9 4.9 slice_add_fusion.1
  43.9 24.1 %scatter-add.6 = f32[5,4,4,4,2,2048]{5,3,2,1,4,0:T(4,128)} dynamic-update-slice(f32[5,4,4,4,2,2048]{5,3,2,1,4,0:T(4,128)} %reshape.210, f32[5,4,4,1,2,2048]{5,3,2,1,4,0:T(1,128)S(1)} %slice_add_fusion.1, s32[]{:T(128)} %constant.145.clone.1, s32[]{:T(128)} %constant.145.clone.1, s32[]{:T(128)} %constant.145.clone.1, s32[]{:T(128)} %constant.145.clone.1, s32[]{:T(128)} %constant.145.clone.1, ...) | dynamic-update-slice | bytes 2621444 | tf_op jit(solution)/shard_map/scatter-add | solution.py:73
  68.0 3.1 fusion.24
  71.1 7.5 %copy.55 = f32[5,4,4,4,2,2048]{5,4,3,2,1,0:T(2,128)S(1)} copy(f32[5,4,4,4,2,2048]{5,3,2,1,4,0:T(4,128)} %fusion.24) | data formatting | bytes 10485760 | tf_op jit(solution)/shard_map/scatter-add | solution.py:74
  78.6 2.3 copy-done.2
  81.9 40.5 %psum.70 = f32[]{:T(128)} all-reduce(f32[]{:T(128)} %multiply_reduce_fusion.9), channel_id=1, replica_groups=mesh['gx'=4,'gy'=8] {'gx','gy'}, use_global_device_ids=true, to_apply=%region_1.0 | all-reduce | flops 1 | bytes 8 | tf_op jit(solution)/shard_map/psum | solution.py:102
  123.1 17.3 %while.32 = (s32[]{:T(128)}, f32[32,320]{1,0:T(8,128)S(1)}, s32[]{:T(128)}, bf16[32,320,320]{2,1,0:T(8,128)(2,1)}, f32[32,320]{1,0:T(8,128)S(1)}, /*index=5*/s32[]{:T(128)}, s32[]{:T(128)}, s32[]{:T(128)}, s32[]{:T(128)}) while((s32[]{:T(128)}, f32[32,320]{1,0:T(8,128)S(1)}, s32[]{:T(128)}, bf16[32,320,320]{2,1,0:T(8,128)(2,1)}, ...), condition=%wide.region_3.4_spmd, body=%wide.region_2.3_spmd.sunk | while | flops 4915206 | bytes 1015959 | solution.py:87
  123.2 2.1 fusion.67
  125.3 2.1 fusion.67
  127.5 2.1 fusion.67
  129.7 2.1 fusion.67
  131.8 2.1 fusion.67
  134.0 2.1 fusion.67
  136.1 2.1 fusion.67
  138.3 2.1 fusion.67
  140.8 3.6 collective-permute-start.3
  144.8 1.4 collective-permute-done.2
  146.9 39.3 %psum.71 = f32[]{:T(128)} all-reduce(f32[]{:T(128)} %get-tuple-element.151), channel_id=1, replica_groups=mesh['gx'=4,'gy'=8] {'gx','gy'}, use_global_device_ids=true, to_apply=%region_5.6 | all-reduce | flops 1 | bytes 8 | tf_op jit(solution)/shard_map/psum | solution.py:123
  187.4 40.7 %psum.72 = f32[]{:T(128)} all-reduce(f32[]{:T(128)} %multiply_reduce_fusion.7), channel_id=1, replica_groups=mesh['gx'=4,'gy'=8] {'gx','gy'}, use_global_device_ids=true, to_apply=%region_7.8 | all-reduce | flops 1 | bytes 8 | tf_op jit(solution)/shard_map/psum | solution.py:126
  229.5 17.3 %while.33 = (s32[]{:T(128)}, f32[32,320]{1,0:T(8,128)S(1)}, s32[]{:T(128)}, bf16[32,320,320]{2,1,0:T(8,128)(2,1)}, f32[32,320]{1,0:T(8,128)S(1)}, /*index=5*/s32[]{:T(128)}, s32[]{:T(128)}, s32[]{:T(128)}, s32[]{:T(128)}) while((s32[]{:T(128)}, f32[32,320]{1,0:T(8,128)S(1)}, s32[]{:T(128)}, bf16[32,320,320]{2,1,0:T(8,128)(2,1)}, ...), condition=%wide.region_9.10_spmd, body=%wide.region_8.9_spmd.sunk | while | flops 4915206 | bytes 1015959 | solution.py:87
  229.5 2.1 fusion.70
  231.7 2.1 fusion.70
  233.8 2.1 fusion.70
  236.0 2.1 fusion.70
  238.2 2.1 fusion.70
  240.3 2.1 fusion.70
  242.5 2.1 fusion.70
  244.6 2.1 fusion.70
  246.9 3.8 collective-permute-start.5
  251.1 1.4 collective-permute-done.4
  253.2 39.5 %psum.73 = f32[]{:T(128)} all-reduce(f32[]{:T(128)} %get-tuple-element.149), channel_id=1, replica_groups=mesh['gx'=4,'gy'=8] {'gx','gy'}, use_global_device_ids=true, to_apply=%region_11.12 | all-reduce | flops 1 | bytes 8 | tf_op jit(solution)/shard_map/psum | solution.py:123
  294.0 6.5 %convert_element_type.82 = bf16[5,64,2,2048]{3,2,1,0:T(2,128)(2,1)} convert(f32[5,64,2,2048]{3,2,1,0:T(2,128)} %bitcast.141) | non-fusion elementwise | flops 1310720 | bytes 7864320 | tf_op jit(solution)/shard_map/convert_element_type | solution.py:92
  300.5 40.6 %psum.74 = f32[]{:T(128)} all-reduce(f32[]{:T(128)} %multiply_reduce_fusion.5), channel_id=1, replica_groups=mesh['gx'=4,'gy'=8] {'gx','gy'}, use_global_device_ids=true, to_apply=%region_13.14 | all-reduce | flops 1 | bytes 8 | tf_op jit(solution)/shard_map/psum | solution.py:123
  341.1 1.9 multiply_reduce_fusion.4
  342.9 40.1 %psum.75 = f32[]{:T(128)} all-reduce(f32[]{:T(128)} %get-tuple-element.147), channel_id=1, replica_groups=mesh['gx'=4,'gy'=8] {'gx','gy'}, use_global_device_ids=true, to_apply=%region_15.16 | all-reduce | flops 1 | bytes 8 | tf_op jit(solution)/shard_map/psum | solution.py:126
  383.7 17.3 %while.34 = (s32[]{:T(128)}, f32[32,320]{1,0:T(8,128)S(1)}, s32[]{:T(128)}, bf16[32,320,320]{2,1,0:T(8,128)(2,1)}, f32[32,320]{1,0:T(8,128)S(1)}, /*index=5*/s32[]{:T(128)}, s32[]{:T(128)}, s32[]{:T(128)}, s32[]{:T(128)}) while((s32[]{:T(128)}, f32[32,320]{1,0:T(8,128)S(1)}, s32[]{:T(128)}, bf16[32,320,320]{2,1,0:T(8,128)(2,1)}, ...), condition=%wide.region_17.18_spmd, body=%wide.region_16.17_spmd.sunk | while | flops 4915206 | bytes 1015959 | solution.py:87
  383.8 2.1 fusion.73
  386.0 2.1 fusion.73
  388.1 2.1 fusion.73
  390.3 2.1 fusion.73
  392.4 2.1 fusion.73
  394.6 2.1 fusion.73
  396.8 2.1 fusion.73
  398.9 2.1 fusion.73
  401.1 2.1 collective-permute-start.6
  403.3 1.7 collective-permute-start.7
  405.4 1.4 collective-permute-done.6
  407.8 39.2 %psum.76 = f32[]{:T(128)} all-reduce(f32[]{:T(128)} %get-tuple-element.145), channel_id=1, replica_groups=mesh['gx'=4,'gy'=8] {'gx','gy'}, use_global_device_ids=true, to_apply=%region_19.20 | all-reduce | flops 1 | bytes 8 | tf_op jit(solution)/shard_map/psum | solution.py:123
  449.0 40.4 %psum.77 = f32[]{:T(128)} all-reduce(f32[]{:T(128)} %multiply_reduce_fusion.2), channel_id=1, replica_groups=mesh['gx'=4,'gy'=8] {'gx','gy'}, use_global_device_ids=true, to_apply=%region_21.22 | all-reduce | flops 1 | bytes 8 | tf_op jit(solution)/shard_map/psum | solution.py:123
  489.4 1.9 multiply_reduce_fusion.1
  491.3 40.2 %psum.78 = f32[]{:T(128)} all-reduce(f32[]{:T(128)} %get-tuple-element.143), channel_id=1, replica_groups=mesh['gx'=4,'gy'=8] {'gx','gy'}, use_global_device_ids=true, to_apply=%region_23.24 | all-reduce | flops 1 | bytes 8 | tf_op jit(solution)/shard_map/psum | solution.py:123
  534.0 40.5 %psum.79 = f32[]{:T(128)} all-reduce(f32[]{:T(128)} %multiply_reduce_fusion), channel_id=1, replica_groups=mesh['gx'=4,'gy'=8] {'gx','gy'}, use_global_device_ids=true, to_apply=%region_25.26 | all-reduce | flops 1 | bytes 8 | tf_op jit(solution)/shard_map/psum | solution.py:126
  575.2 2.0 maximum_bitcast_fusion.2
  580.4 2.5 multiply_add_fusion
  (129 shorter events, 22.4 us)
Async XLA Ops:
  0.6 24.6 %copy-start = (bf16[3,64,64]{2,1,0:T(8,128)(2,1)S(1)}, bf16[3,64,64]{2,1,0:T(8,128)(2,1)}, u32[]{:S(2)}) copy-start(bf16[3,64,64]{2,1,0:T(8,128)(2,1)} %param.18) | copy-start | bytes 73732
  0.6 11.3 %copy-start.1 = (bf16[5,64,2,2048]{3,2,1,0:T(2,128)(2,1)S(1)}, bf16[5,64,2,2048]{3,2,1,0:T(2,128)(2,1)}, u32[]{:S(2)}) copy-start(bf16[5,64,2,2048]{3,2,1,0:T(2,128)(2,1)} %param.17) | copy-start | bytes 7864324
  2.0 36.4 %collective-permute-start = (bf16[5,4,4,2]{0,2,3,1:T(4,128)(2,1)S(1)}, bf16[5,4,4,2]{0,2,3,1:T(4,128)(2,1)S(1)}, u32[]{:S(2)}, u32[]{:S(2)}) collective-permute-start(bf16[5,4,4,2]{0,2,3,1:T(4,128)(2,1)S(1)} %bitcast.143), channel_id=1, source_target_pairs={{0,8},{8,16},{16,24},{24,0},{1,9},{9,17},{17,25},{25,1},{2,10},{10... | collective-permute-start | bytes 968 | tf_op jit(solution)/shard_map/ppermute | solution.py:20
  9.8 58.2 %collective-permute-start.1 = (bf16[5,4,4,2048]{3,2,1,0:T(4,128)(2,1)}, bf16[5,4,4,2048]{3,2,1,0:T(4,128)(2,1)}, u32[]{:S(2)}, u32[]{:S(2)}) collective-permute-start(bf16[5,4,4,2048]{3,2,1,0:T(4,128)(2,1)} %bitcast.120), channel_id=1, source_target_pairs={{0,1},{1,2},{2,3},{3,4},{4,5},{5,6},{6,7},{8,9},{9,10},{10,11},{11... | collective-permute-start | bytes 983048 | tf_op jit(solution)/shard_map/ppermute | solution.py:26
  28.6 7.2 %copy-start.4 = (bf16[5,4,4,1,2,2047]{5,4,3,2,1,0:T(2,128)(2,1)S(1)}, bf16[5,4,4,1,2,2047]{5,4,3,2,1,0:T(2,128)(2,1)}, u32[]{:S(2)}) copy-start(bf16[5,4,4,1,2,2047]{5,4,3,2,1,0:T(2,128)(2,1)} %slice.152) | copy-start | bytes 1965124
  28.6 8.7 %copy-start.3 = (bf16[5,4,1,4,1,2048]{5,4,3,2,1,0:T(2,128)(2,1)S(1)}, bf16[5,4,1,4,1,2048]{5,4,3,2,1,0:T(2,128)(2,1)}, u32[]{:S(2)}) copy-start(bf16[5,4,1,4,1,2048]{5,4,3,2,1,0:T(2,128)(2,1)} %get-tuple-element.157) | copy-start | bytes 983044
  43.9 24.1 %copy-start.5 = (bf16[5,4,1,4,2,2048]{5,4,3,2,1,0:T(2,128)(2,1)S(1)}, bf16[5,4,1,4,2,2048]{5,4,3,2,1,0:T(2,128)(2,1)}, u32[]{:S(2)}) copy-start(bf16[5,4,1,4,2,2048]{5,4,3,2,1,0:T(2,128)(2,1)} %slice.157) | copy-start | bytes 1966084
  43.9 24.1 %copy-start.6 = (bf16[5,4,1,4,1,2048]{5,3,2,1,4,0:T(4,128)(2,1)S(1)}, bf16[5,4,1,4,1,2048]{5,3,2,1,4,0:T(4,128)(2,1)}, u32[]{:S(2)}) copy-start(bf16[5,4,1,4,1,2048]{5,3,2,1,4,0:T(4,128)(2,1)} %copy.78) | copy-start | bytes 983044
  71.1 10.0 %copy-start.9 = (f32[32,320]{1,0:T(8,128)S(1)}, f32[32,320]{1,0:T(8,128)}, u32[]{:S(2)}) copy-start(f32[32,320]{1,0:T(8,128)} %param.20) | copy-start | bytes 122884
  78.6 2.3 copy-start.2
  123.1 21.3 %copy-start.8 = (f32[64,64]{1,0:T(8,128)S(1)}, f32[64,64]{1,0:T(8,128)}, u32[]{:S(2)}) copy-start(f32[64,64]{1,0:T(8,128)} %param.19) | copy-start | bytes 49156
  123.1 23.1 %copy-start.7 = (f32[32,320]{1,0:T(8,128)S(1)}, f32[32,320]{1,0:T(8,128)}, u32[]{:S(2)}) copy-start(f32[32,320]{1,0:T(8,128)} %param.21) | copy-start | bytes 122884
  140.5 5.7 collective-permute-start.2
  140.8 5.4 collective-permute-start.3
  246.9 5.7 collective-permute-start.4
  246.9 5.6 collective-permute-start.5
  401.1 5.7 collective-permute-start.6
  403.3 3.8 collective-permute-start.7
where the time goes:
time: 586 us; the launch traced here: 583 us
  blocking collectives  401 us (68%)
  local copies, waits for them, and re-layouts  56 us (10%)
  matrix products  55.2 us (9%)
  other arithmetic  44.4 us (8%)
  starting transfers between devices  16.9 us (3%)
    psum x6, blocking collectives, per_device(): value = lax.psum(jnp.sum(image * basis[row_index]), ('gx', 'gy'))  239 us
    psum x3, blocking collectives, per_device(): length = jnp.sqrt(lax.psum(jnp.sum(image * image), ('gx', 'gy')))  121 us
    dot_general x24, matrix products, one_group(): jnp.einsum('gij,gj->gi', block, piece, precision=lax.Precision.HIGHEST)  50.8 us
    psum x1, blocking collectives, per_device(): beta = jnp.sqrt(lax.psum(jnp.sum(rhs * rhs), ('gx', 'gy')))  40.5 us
    scatter-add x1, local copies, waits for them, and re-layouts, explicit_residual(): resid = resid.at[:, :, :, 0].add(upwind_x * jump_x)  24.1 us
  transfers between devices with their start and end apart: 8, of which 4 were waited for; matrix products, arithmetic and copies ran while one was open for 10% of the time, Pallas kernels for 0%

commit v1 on v0

v1 whole, which is shorter than its diff:
```python
import jax
import jax.numpy as jnp
import numpy as np
from jax import lax
from jax.experimental import pallas as pl
from jax.experimental.pallas import tpu as pltpu
from jax.sharding import PartitionSpec as P

Q = 4
ITERS = 3

time_step = 0.3
coupling = 0.25
upwind_x = 2.0
upwind_y = 1.0
advection = (1.0, 0.5, 0.25)

LANES = 128
GROUP = 8
VMEM_BYTES = 24 << 20
bf16 = jnp.bfloat16
f32 = jnp.float32

in_vmem = pl.BlockSpec(memory_space=pltpu.VMEM)
in_hbm = pl.BlockSpec(memory_space=pltpu.HBM)
in_smem = pl.BlockSpec(memory_space=pltpu.SMEM)
params = pltpu.CompilerParams(vmem_limit_bytes=VMEM_BYTES)


def held_in_hbm(array):
    return pltpu.with_memory_space_constraint(array, pltpu.HBM)


def ring(axis, by):
    count = lax.axis_size(axis)
    return [(i, (i + by) % count) for i in range(count)]


def from_below(array, axis):
    count = lax.axis_size(axis)
    return lax.ppermute(array, axis, [(i, i + 1) for i in range(count - 1)])


def neighbours(array, axis):
    count = lax.axis_size(axis)
    if count % 2 or count < 4:
        return lax.ppermute(array, axis, ring(axis, 1)), lax.ppermute(array, axis, ring(axis, -1))
    even = [(i, i ^ 1) for i in range(count)]
    odd = [(i, (i + (1 if i % 2 else -1)) % count) for i in range(count)]
    return lax.ppermute(array, axis, even), lax.ppermute(array, axis, odd)


def jump_matrix(nodes, rows):
    faces = nodes // Q
    out = np.zeros((nodes * rows, nodes * rows + 2 * faces * rows), np.float32)
    for m in range(nodes):
        i, j, k = m % Q, m // Q % Q, m // (Q * Q)
        for r in range(rows):
            row = m * rows + r
            if i == 0:
                out[row, row] -= upwind_x
                out[row, nodes * rows + (m // Q) * rows + r] += upwind_x
            if j == 0:
                out[row, row] -= upwind_y
                if r > 0:
                    out[row, (m + Q * (Q - 1)) * rows + r - 1] += upwind_y
                else:
                    column = (k * Q + i) * rows + rows - 1
                    out[row, (nodes + faces) * rows + column] += upwind_y
    return out


def tile_view(array):
    *lead, rows, cols = array.shape
    return jnp.swapaxes(array.reshape(*lead, rows, cols // LANES, LANES), -3, -2)


def from_tile_view(array):
    *lead, tiles, rows, lanes = array.shape
    return jnp.swapaxes(array, -3, -2).reshape(*lead, rows, tiles * lanes)


def faces_kernel(state_ref, edge_ref, corner_ref, top_ref, sem):
    comps, _, _, tiles, rows, lanes = state_ref.shape
    top = [
        pltpu.make_async_copy(
            state_ref.at[:, pl.ds(k * Q + Q - 1, 1), :, t], top_ref.at[t, :, pl.ds(k, 1)], sem.at[2 + Q + t * Q + k]
        )
        for t in range(tiles)
        for k in range(Q)
    ]
    copies = [pltpu.make_async_copy(state_ref.at[:, :, Q - 1, tiles - 1], edge_ref, sem.at[0])]
    copies += [
        pltpu.make_async_copy(
            state_ref.at[:, pl.ds(k * Q + Q - 1, 1), :, 0], corner_ref.at[:, pl.ds(k, 1)], sem.at[1 + k]
        )
        for k in range(Q)
    ]
    for copy in copies + top:
        copy.start()
    for copy in copies + top:
        copy.wait()


def prep_kernel(
    state_ref, blocks_ref, rhs_ref, sigma_ref, deriv_ref, stiff_ref, expand_ref, jump_ref,
    tiles_ref, blocks_out_ref, rhs_out_ref, sigma_out_ref, full_ref, first_ref, block_ref,
    deriv_in, stiff_in, expand_in, jump_in, sem,
):
    count = tiles_ref.shape[0]
    small = [
        pltpu.make_async_copy(source, target, sem.at[at])
        for at, (source, target) in enumerate([
            (deriv_ref, deriv_in), (expand_ref, expand_in), (jump_ref, jump_in), (stiff_ref, stiff_in),
            (rhs_ref, rhs_out_ref), (sigma_ref, sigma_out_ref), (blocks_ref, blocks_out_ref),
        ])
    ]
    large = [
        pltpu.make_async_copy(state_ref.at[:, :, :, t], tiles_ref.at[t], sem.at[len(small) + t]) for t in range(count)
    ]
    for copy in small[:-1] + large + small[-1:]:
        copy.start()
    for copy in small[:4]:
        copy.wait()
    size, nodes = expand_in.shape
    rows = size // nodes
    expand = expand_in[...]
    same = lax.broadcasted_iota(jnp.int32, (size, size), 0) % rows
    same = same == lax.broadcasted_iota(jnp.int32, (size, size), 1) % rows
    own = lax.broadcasted_iota(jnp.int32, (nodes, size), 1) % rows == 0
    for d in range(3):
        wide = lax.dot_general(
            deriv_in[d], expand, (((1,), (1,)), ((), ())), preferred_element_type=f32
        ).astype(bf16)
        both = jnp.dot(expand, wide, preferred_element_type=f32)
        full_ref[:, d * size : (d + 1) * size] = jnp.where(same, both, 0.0).astype(bf16)
        first_ref[:, d * size : (d + 1) * size] = jnp.where(own, wide.astype(f32), 0.0).astype(bf16)
    full_ref[:, 3 * size :] = jump_in[:size]
    first_ref[:, 3 * size :] = jump_in[size:]
    block_ref[...] = jnp.zeros_like(block_ref)
    high, low = split(stiff_in[...])
    for v in range(block_ref.shape[1] // nodes):
        at = slice(v * nodes, (v + 1) * nodes)
        block_ref[0, at, at] = high
        block_ref[1, at, at] = low
    for copy in small[4:-1] + large + small[-1:]:
        copy.wait()


def fill_columns(stack_ref, speed_ref, own_at, last_at, edge_at, top_at, comps):
    size, width = speed_ref.shape[1:]
    face = size // Q
    for d in range(3):
        speed_ref[d] = advection[d] + own_at(1 + d).astype(f32)
    lane = lax.broadcasted_iota(jnp.int32, (face, width), 1)
    for v in range(comps):
        own = own_at(v)
        wide = own.astype(f32)
        for d in range(3):
            stack_ref[d * size : (d + 1) * size] = (wide * speed_ref[d]).astype(bf16)
        stack_ref[3 * size : 4 * size] = own
        last = pltpu.roll(last_at(v).astype(f32), 1, 1)
        edge = pltpu.roll(edge_at(v).astype(f32), 1, 1)
        edge = jnp.concatenate([edge] * (width // LANES), axis=1)
        stack_ref[4 * size : 4 * size + face] = jnp.where(lane == 0, edge, last).astype(bf16)
        stack_ref[4 * size + face :] = top_at(v)
        yield v


def outer_piece(tiles, edge, top, full, after, result, start, stop, width):
    count, comps, faces, _, rows, _ = tiles.shape
    size = faces * Q * rows
    face = faces * rows
    per_step = width // LANES
    held = (stop - start) * per_step
    shape = (comps, faces, Q, count, rows, LANES)

    def kernel(tiles_ref, edge_ref, top_ref, full_ref, *refs):
        out_ref, done_ref, stack_ref, speed_ref, held_ref, sem = refs[-6:]
        done_ref[...] = jnp.zeros_like(done_ref)

        def joined(read, height):
            return jnp.concatenate([read(k).reshape(height, LANES) for k in range(per_step)], axis=1)

        def copy(i):
            return pltpu.make_async_copy(
                held_ref.at[i], out_ref.at[:, :, :, start * per_step + i], sem.at[i]
            )

        def step(n, carry):
            base = (start + n) * per_step
            columns = fill_columns(
                stack_ref, speed_ref,
                lambda v: joined(lambda k: tiles_ref[base + k, v], size),
                lambda v: joined(lambda k: tiles_ref[base + k, v, :, Q - 1], face),
                lambda v: jnp.where(
                    base == 0,
                    edge_ref[v].reshape(face, LANES).astype(f32),
                    tiles_ref[jnp.maximum(base - 1, 0), v, :, Q - 1].reshape(face, LANES).astype(f32),
                ),
                lambda v: joined(lambda k: top_ref[base + k, v], face),
                comps,
            )
            for v in columns:
                value = jnp.dot(full_ref[...], stack_ref[...], preferred_element_type=f32).astype(bf16)
                for k in range(per_step):
                    part = value[:, k * LANES : (k + 1) * LANES].reshape(faces, Q, rows, LANES)
                    held_ref[n * per_step + k, v] = part
            for k in range(per_step):
                copy(n * per_step + k).start()
            return carry

        lax.fori_loop(0, stop - start, step, 0)
        for i in range(held):
            copy(i).wait()

    operands = [tiles, edge, top, full, after]
    specs = [in_vmem] * 5
    aliases = {}
    if result is not None:
        operands.append(held_in_hbm(result))
        specs.append(in_hbm)
        aliases = {5: 0}
    return pl.pallas_call(
        kernel,
        in_specs=specs,
        out_specs=[in_hbm, in_vmem],
        out_shape=[pltpu.HBM(shape, bf16), jax.ShapeDtypeStruct((8, LANES), f32)],
        scratch_shapes=[
            pltpu.VMEM((full.shape[1], width), bf16),
            pltpu.VMEM((3, size, width), f32),
            pltpu.VMEM((held, comps, faces, Q, rows, LANES), bf16),
            pltpu.SemaphoreType.DMA((held,)),
        ],
        input_output_aliases=aliases,
        compiler_params=params,
        name="outer",
    )(*operands)


def split(value):
    high = value.astype(bf16)
    return high, (value - high.astype(f32)).astype(bf16)


def whole(reduce, value):
    return reduce(reduce(value, axis=0, keepdims=True), axis=1, keepdims=True)


def rescale(value):
    top = whole(jnp.max, jnp.abs(value))
    by = jnp.where(top > 0.0, jnp.ceil(jnp.log2(jnp.maximum(top, 1e-37))), 0.0)
    return value * jnp.exp2(-by), by


def apply_blocks(count, value_ref, blocks_ref, out_ref):
    _, order = value_ref.shape
    rows = lax.broadcasted_iota(jnp.int32, (2 * GROUP, order), 0)
    out_ref[...] = jnp.zeros_like(out_ref)

    def group(g, carry):
        base = pl.multiple_of(g * GROUP, GROUP)
        terms = jnp.concatenate(split(value_ref[pl.ds(base, GROUP), :]), axis=0)
        kept = jnp.zeros((2 * GROUP, order), f32)
        for s in range(GROUP):
            product = lax.dot_general(
                terms, blocks_ref[base + s], (((1,), (1,)), ((), ())), preferred_element_type=f32
            )
            kept = jnp.where((rows == s) | (rows == s + GROUP), product, kept)
        out_ref[pl.ds(base, GROUP), :] = kept[:GROUP] + kept[GROUP:]
        return carry

    lax.fori_loop(0, (count + GROUP - 1) // GROUP, group, 0)


def emit(direction_ref, exponent, sent_ref, exponent_ref):
    slots, order = direction_ref.shape
    exponent_ref[...] = jnp.broadcast_to(exponent, exponent_ref.shape)
    sent_ref[:, :order] = direction_ref[...].astype(bf16)
    sent_ref[:, order:] = jnp.broadcast_to(exponent, (slots, sent_ref.shape[1] - order)).astype(bf16)


def live_rows(count, shape):
    return (lax.broadcasted_iota(jnp.int32, shape, 0) < count).astype(f32)


def start_kernel(
    count_ref, tiles_ref, edge_ref, corner_ref, first_ref, rhs_ref, blocks_ref,
    basis_ref, direction_ref, sent_ref, exponent_ref, stack_ref, speed_ref, trace_ref,
):
    slots, order = rhs_ref.shape
    _, comps, faces, _, rows, _ = tiles_ref.shape
    nodes = order // comps
    size, face = nodes * rows, faces * rows
    columns = fill_columns(
        stack_ref, speed_ref,
        lambda v: tiles_ref[0, v].reshape(size, LANES),
        lambda v: tiles_ref[0, v, :, Q - 1].reshape(face, LANES),
        lambda v: edge_ref[v].reshape(face, LANES),
        lambda v: corner_ref[v].reshape(face, LANES),
        comps,
    )
    for v in columns:
        value = jnp.dot(first_ref[...], stack_ref[...], preferred_element_type=f32)
        trace_ref[:, v * nodes : (v + 1) * nodes] = value.T[:slots]
    count = count_ref[0, 0]
    rhs = live_rows(count, rhs_ref.shape) * (rhs_ref[...] + time_step * trace_ref[...])
    basis, exponent = rescale(rhs)
    basis_ref[...] = basis
    apply_blocks(count, basis_ref, blocks_ref, direction_ref)
    emit(direction_ref, exponent, sent_ref, exponent_ref)


def operate(count_ref, direction_ref, exponent_ref, one_ref, two_ref, sigma_ref, stiff_ref):
    slots, order = direction_ref.shape
    direction = direction_ref[...]
    high, low = split(direction)
    both = jnp.dot(jnp.concatenate([high, low], axis=0), stiff_ref[0], preferred_element_type=f32)
    stiff = both[:slots] + both[slots:] + jnp.dot(high, stiff_ref[1], preferred_element_type=f32)
    exponent = exponent_ref[0:1, 0:1]
    exponent_one = jnp.max(one_ref[0:1, order:].astype(f32), axis=1, keepdims=True)
    exponent_two = jnp.max(two_ref[0:1, order:].astype(f32), axis=1, keepdims=True)
    common = jnp.maximum(exponent, jnp.maximum(exponent_one, exponent_two))
    own = direction + time_step * (sigma_ref[...] * direction + stiff)
    one = one_ref[:, :order].astype(f32) * jnp.exp2(exponent_one - common)
    two = two_ref[:, :order].astype(f32) * jnp.exp2(exponent_two - common)
    image = own * jnp.exp2(exponent - common) - coupling * (one + two)
    basis, by = rescale(live_rows(count_ref[0, 0], image.shape) * image)
    return basis, common + by


def middle_kernel(
    count_ref, previous_ref, previous_exponent_ref, one_ref, two_ref, sigma_ref, stiff_ref, blocks_ref, _,
    basis_ref, direction_ref, sent_ref, exponent_ref,
):
    basis, exponent = operate(
        count_ref, previous_ref, previous_exponent_ref, one_ref, two_ref, sigma_ref, stiff_ref
    )
    basis_ref[...] = basis
    apply_blocks(count_ref[0, 0], basis_ref, blocks_ref, direction_ref)
    emit(direction_ref, exponent, sent_ref, exponent_ref)


def pairs():
    return [(k, l) for k in range(ITERS + 1) for l in range(k, ITERS + 1)]


def gram_kernel(count_ref, _, previous_ref, *refs):
    exponent_refs, refs = refs[:ITERS], refs[ITERS:]
    one_ref, two_ref, sigma_ref, stiff_ref = refs[:4]
    basis_refs, part_ref = refs[4:-1], refs[-1]
    last, exponent = operate(
        count_ref, previous_ref, exponent_refs[-1], one_ref, two_ref, sigma_ref, stiff_ref
    )
    basis = [ref[...] for ref in basis_refs] + [last]
    lane = lax.broadcasted_iota(jnp.int32, (1, LANES), 1)
    row = jnp.zeros((1, LANES), f32)
    values = [whole(jnp.sum, basis[k] * basis[l]) for k, l in pairs()]
    values += [ref[0:1, 0:1] for ref in exponent_refs] + [exponent]
    for at, value in enumerate(values):
        row = jnp.where(lane == at, value, row)
    part_ref[...] = jnp.broadcast_to(row[None], part_ref.shape)


def finish_kernel(parts_ref, *refs):
    exponent_refs, direction_refs, out_ref = refs[:ITERS], refs[ITERS:-1], refs[-1]
    parts = parts_ref[:, 0, :]
    index = {pair: at for at, pair in enumerate(pairs())}
    count = ITERS + 1
    exponents = [parts[:, len(index) + k : len(index) + k + 1] for k in range(count)]
    tops = [jnp.max(e, axis=0, keepdims=True) for e in exponents]
    factors = [jnp.exp2(e - top) for e, top in zip(exponents, tops)]
    gram = {
        (k, l): jnp.sum(parts[:, at : at + 1] * factors[k] * factors[l], axis=0, keepdims=True)
        for (k, l), at in index.items()
    }
    scale = [lax.rsqrt(jnp.maximum(gram[k, k], 1e-37)) for k in range(count)]
    matrix = {(k, l): gram[k, l] * scale[k] * scale[l] for k, l in index}
    lower, inverse, middle = {}, [], []
    for k in range(ITERS):
        pivot = matrix[k + 1, k + 1]
        right = matrix[0, k + 1]
        for p in range(k):
            pivot = pivot - lower[k, p] * lower[k, p]
            right = right - lower[k, p] * middle[p]
        inverse.append(jnp.where(pivot > 5e-7, lax.rsqrt(jnp.maximum(pivot, 5e-7)), 0.0))
        for l in range(k + 1, ITERS):
            value = matrix[k + 1, l + 1]
            for p in range(k):
                value = value - lower[l, p] * lower[k, p]
            lower[l, k] = value * inverse[k]
        middle.append(right * inverse[k])
    weights = [None] * ITERS
    for k in reversed(range(ITERS)):
        value = middle[k]
        for l in range(k + 1, ITERS):
            value = value - lower[l, k] * weights[l]
        weights[k] = value * inverse[k]
    norm = gram[0, 0] * scale[0]
    total = None
    for k in range(ITERS):
        shift = jnp.exp2(tops[0] - tops[k + 1] + exponent_refs[k][0:1, 0:1])
        term = (weights[k] * scale[k + 1] * norm * shift) * direction_refs[k][...]
        total = term if total is None else total + term
    out_ref[...] = total


def per_device(outer_state, derivative, stiffness, wall_rhs, wall_sigma, wall_inverse, wall_count):
    comps, nodes, rows, cols = outer_state.shape
    slots, order = wall_rhs.shape
    faces = nodes // Q
    size = nodes * rows
    state = held_in_hbm(tile_view(outer_state.reshape(comps, faces, Q, rows, cols)))
    count = cols // LANES
    edge_shape = jax.ShapeDtypeStruct((comps, faces, rows, LANES), bf16)
    corner_shape = jax.ShapeDtypeStruct((comps, Q, Q, rows, LANES), bf16)

    edge, corner, top = pl.pallas_call(
        faces_kernel,
        in_specs=[in_hbm],
        out_specs=[in_vmem] * 3,
        out_shape=[edge_shape, corner_shape, jax.ShapeDtypeStruct((count, *corner_shape.shape), bf16)],
        scratch_shapes=[pltpu.SemaphoreType.DMA((2 + Q + count * Q,))],
        compiler_params=params,
        name="faces",
    )(state)
    came_edge = lax.ppermute(edge, "gx", ring("gx", 1))
    came_corner = from_below(corner, "gy")
    came_top = from_below(top, "gy")

    jumps = jump_matrix(nodes, rows)
    depth = 3 * size + jumps.shape[1]
    expand = np.repeat(np.eye(nodes, dtype=np.float32), rows, axis=0)
    jumps = np.concatenate([jumps, jumps[::rows]])
    operands = (
        state, wall_inverse, wall_rhs, wall_sigma, derivative, stiffness, jnp.asarray(expand, bf16),
        jnp.asarray(jumps, bf16),
    )
    operands = tuple(held_in_hbm(operand) for operand in operands)
    tiles, blocks, rhs, sigma, full, first, stiff = pl.pallas_call(
        prep_kernel,
        in_specs=[in_hbm] * len(operands),
        out_specs=[in_vmem] * 7,
        out_shape=[
            jax.ShapeDtypeStruct((count, comps, faces, Q, rows, LANES), bf16),
            jax.ShapeDtypeStruct(wall_inverse.shape, bf16),
            jax.ShapeDtypeStruct(wall_rhs.shape, f32),
            jax.ShapeDtypeStruct(wall_sigma.shape, f32),
            jax.ShapeDtypeStruct((size, depth), bf16),
            jax.ShapeDtypeStruct((nodes, depth), bf16),
            jax.ShapeDtypeStruct((2, order, order), bf16),
        ],
        scratch_shapes=[pltpu.VMEM(a.shape, a.dtype) for a in (derivative, stiffness)]
        + [pltpu.VMEM(expand.shape, bf16), pltpu.VMEM(jumps.shape, bf16), pltpu.SemaphoreType.DMA((7 + count,))],
        compiler_params=params,
        name="prep",
    )(*operands)

    vector = jax.ShapeDtypeStruct((slots, order), f32)
    padded = -(-(order + 1) // LANES) * LANES
    step_shapes = [
        vector, vector, jax.ShapeDtypeStruct((slots, padded), bf16), jax.ShapeDtypeStruct((8, LANES), f32),
    ]
    basis, direction, sent, exponent = pl.pallas_call(
        start_kernel,
        in_specs=[in_smem] + [in_vmem] * 6,
        out_specs=[in_vmem] * 4,
        out_shape=step_shapes,
        scratch_shapes=[
            pltpu.VMEM((depth, LANES), bf16), pltpu.VMEM((3, size, LANES), f32), pltpu.VMEM((slots, order), f32),
        ],
        compiler_params=params,
        name="start",
    )(wall_count, tiles, came_edge, came_corner, first, rhs, blocks)
    bases, directions, exponents = [basis], [direction], [exponent]

    width = 2 * LANES
    steps = cols // width
    bounds = [steps * k // ITERS for k in range(ITERS + 1)]
    residual = None
    for k in range(ITERS):
        one, two = neighbours(sent, "gx")
        residual, done = outer_piece(
            tiles, came_edge, came_top, full, exponent, residual, bounds[k], bounds[k + 1], width
        )
        if k < ITERS - 1:
            basis, direction, sent, exponent = pl.pallas_call(
                middle_kernel,
                in_specs=[in_smem] + [in_vmem] * 8,
                out_specs=[in_vmem] * 4,
                out_shape=step_shapes,
                compiler_params=params,
                name="middle",
            )(wall_count, direction, exponent, one, two, sigma, stiff, blocks, done)
            bases.append(basis)
            directions.append(direction)
            exponents.append(exponent)

    devices = lax.axis_size("gx") * lax.axis_size("gy")
    part = pl.pallas_call(
        gram_kernel,
        in_specs=[in_smem] + [in_vmem] * (6 + 2 * ITERS),
        out_specs=in_vmem,
        out_shape=jax.ShapeDtypeStruct((devices, 1, LANES), f32),
        compiler_params=params,
        name="gram",
    )(wall_count, done, direction, *exponents, one, two, sigma, stiff, *bases)
    parts = lax.all_to_all(part, ("gx", "gy"), 0, 0)
    wall_update = pl.pallas_call(
        finish_kernel,
        in_specs=[in_vmem] * (1 + 2 * ITERS),
        out_specs=in_vmem,
        out_shape=vector,
        compiler_params=params,
        name="finish",
    )(parts, *exponents, *directions)
    return from_tile_view(residual).reshape(outer_state.shape), wall_update


def solution(mesh):
    in_specs = (
        P(None, None, "gy", "gx"),
        P(),
        P(),
        P(("gx", "gy"), None),
        P(("gx", "gy"), None),
        P(("gx", "gy"), None, None),
        P("gx", "gy"),
    )
    out_specs = (P(None, None, "gy", "gx"), P(("gx", "gy"), None))
    return jax.shard_map(
        per_device, mesh=mesh, in_specs=in_specs, out_specs=out_specs, check_vma=False
    )
```

time: 586 us -> 55.9 us (0.10)
  blocking collectives: 401 us -> 9.16 us
  local copies, waits for them, and re-layouts: 56 us -> 0 us
  matrix products: 55.2 us -> 0 us
  other arithmetic: 44.4 us -> 0 us
  Pallas kernels: 0 us -> 27 us
    psum x10 -> x0, blocking collectives: 401 us -> none  [the longest x6 239 us: per_device(): value = lax.psum(jnp.sum(image * basis[row_index]), ('gx', 'gy'))]
    dot_general x29 -> x0, matrix products: 54.9 us -> none  [the longest x24 50.8 us: one_group(): jnp.einsum('gij,gj->gi', block, piece, precision=lax.Precision.HIGHEST)]
    scatter-add x2 -> x0, local copies, waits for them, and re-layouts: 31.6 us -> none  [the longest x1 24.1 us: explicit_residual(): resid = resid.at[:, :, :, 0].add(upwind_x * jump_x)]
    pallas_call x0 -> x10, Pallas kernels: none -> 27 us  [the longest x3 8.74 us: outer_piece(): pl.pallas_call(kernel, in_specs=specs, out_specs=[in_hbm, in_vmem], out_s...]
    reduce_sum x10 -> x0, other arithmetic: 11.5 us -> none  [the longest x6 6.43 us: per_device(): value = lax.psum(jnp.sum(image * basis[row_index]), ('gx', 'gy'))]
    convert_element_type x6 -> x0, other arithmetic: 10.1 us -> none  [the longest x1 6.53 us: per_device(): outer_residual = resid.astype(jnp.bfloat16)]
    all_to_all x0 -> x1, blocking collectives: none -> 9.16 us  [per_device(): parts = lax.all_to_all(part, ('gx', 'gy'), 0, 0)]
    slice x6 -> x0, local copies, waits for them, and re-layouts: 9.13 us -> none  [the longest x1 3.72 us: explicit_residual(): top_row = cube[:, :, Q - 1, :, rows - 1, :]]
  transfers between devices with their start and end apart: 8 -> 9, of which waited for: 4 -> 6; matrix products, arithmetic and copies ran while one was open for 10% -> 0% of each run, Pallas kernels for 0% -> 31%
where the time goes in v1:
time: 55.9 us; the launch traced here: 55.6 us
  Pallas kernels  27 us (48%)
  starting transfers between devices  15.2 us (27%)
  blocking collectives  9.16 us (16%)
  waiting for transfers between devices  2.91 us (5%)
  between operations  1.39 us (2%)
    all_to_all x1, blocking collectives, per_device(): parts = lax.all_to_all(part, ('gx', 'gy'), 0, 0)  9.16 us
    pallas_call x3, Pallas kernels, outer_piece(): pl.pallas_call(kernel, in_specs=specs, out_specs=[in_hbm, in_vmem], out_s...  8.74 us
    ppermute x6, starting transfers between devices, neighbours(): return (lax.ppermute(array, axis, even), lax.ppermute(array, axis, odd))  6.97 us
    pallas_call x2, Pallas kernels, per_device(): pl.pallas_call(middle_kernel, in_specs=[in_smem] + [in_vmem] * 8, out_spe...  6.01 us
    ppermute x2, starting transfers between devices, from_below(): return lax.ppermute(array, axis, [(i, i + 1) for i in range(count - 1)])  5.79 us
    pallas_call x1, Pallas kernels, per_device(): pl.pallas_call(prep_kernel, in_specs=[in_hbm] * len(operands), out_specs=...  4.75 us
    pallas_call x1, Pallas kernels, per_device(): pl.pallas_call(start_kernel, in_specs=[in_smem] + [in_vmem] * 6, out_spec...  3.76 us
    ppermute x6, waiting for transfers between devices, neighbours(): return (lax.ppermute(array, axis, even), lax.ppermute(array, axis, odd))  2.9 us
  transfers between devices with their start and end apart: 9, of which 6 were waited for; matrix products, arithmetic and copies ran while one was open for 0% of the time, Pallas kernels for 31%

profile of v1, /device:TPU:0, one launch (start us, length us, event | category | flops | bytes accessed | tf_op | source)
XLA Modules:
  0.0 55.6 jit_solution(8422036293873846804)
XLA Ops:
  0.6 1.8 %faces.1 = (bf16[5,16,2,128]{3,2,1,0:T(2,128)(2,1)S(1)}, bf16[5,4,4,2,128]{4,3,2,1,0:T(2,128)(2,1)S(1)}, bf16[16,5,4,4,2,128]{5,4,3,2,1,0:T(2,128)(2,1)S(1)}) custom-call(bf16[5,16,4,16,2,128]{5,4,3,2,1,0:T(2,128)(2,1)} %bitcast.7), custom_call_target="tpu_custom_call" | custom-call | tf_op jit(solution)/shard_map/faces/pallas_call | solution.py:418
  2.4 2.4 %collective-permute-start.1 = (bf16[16,5,4,4,2,128]{5,4,3,2,1,0:T(2,128)(2,1)S(1)}, bf16[16,5,4,4,2,128]{5,4,3,2,1,0:T(2,128)(2,1)S(1)}, u32[]{:S(2)}, u32[]{:S(2)}) collective-permute-start(bf16[16,5,4,4,2,128]{5,4,3,2,1,0:T(2,128)(2,1)S(1)} %get-tuple-element.32), channel_id=1, source_target_pairs={{0,1},{1,2},{2,3},{3,4},{4,5},{5,6},{6,7},{8,9},{9,10},{10,11},{11... | collective-permute-start | bytes 1966088 | tf_op jit(solution)/shard_map/ppermute | solution.py:41
  4.9 2.4 %collective-permute-start = (bf16[5,16,2,128]{3,2,1,0:T(2,128)(2,1)S(1)}, bf16[5,16,2,128]{3,2,1,0:T(2,128)(2,1)S(1)}, u32[]{:S(2)}, u32[]{:S(2)}) collective-permute-start(bf16[5,16,2,128]{3,2,1,0:T(2,128)(2,1)S(1)} %get-tuple-element.31), channel_id=1, source_target_pairs={{0,8},{8,16},{16,24},{24,0},{1,9},{9,17},{17,25},{25,1},{2,10},{10... | collective-permute-start | bytes 122888 | tf_op jit(solution)/shard_map/ppermute | solution.py:427
  7.3 3.3 %collective-permute-start.2 = (bf16[5,4,4,2,128]{4,3,2,1,0:T(2,128)(2,1)S(1)}, bf16[5,4,4,2,128]{4,3,2,1,0:T(2,128)(2,1)S(1)}, u32[]{:S(2)}, u32[]{:S(2)}) collective-permute-start(bf16[5,4,4,2,128]{4,3,2,1,0:T(2,128)(2,1)S(1)} %get-tuple-element.34), channel_id=1, source_target_pairs={{0,1},{1,2},{2,3},{3,4},{4,5},{5,6},{6,7},{8,9},{9,10},{10,11},{11... | collective-permute-start | bytes 122888 | tf_op jit(solution)/shard_map/ppermute | solution.py:41
  11.3 4.7 %prep.1 = (bf16[16,5,16,4,2,128]{5,4,3,2,1,0:T(2,128)(2,1)S(1)}, bf16[32,320,320]{2,1,0:T(8,128)(2,1)S(1)}, f32[32,320]{1,0:T(8,128)S(1)}, f32[32,320]{1,0:T(8,1...) custom-call(bf16[5,16,4,16,2,128]{5,4,3,2,1,0:T(2,128)(2,1)} %bitcast.8, ...), custom_call_target="tpu_custom_call" | custom-call | tf_op jit(solution)/shard_map/prep/pallas_call | solution.py:440
  16.1 0.0 collective-permute-done.edge_ref
  16.1 0.0 collective-permute-done.2.corner_ref
  16.1 3.8 %start.1 = (f32[32,320]{1,0:T(8,128)S(1)}, f32[32,320]{1,0:T(8,128)S(1)}, bf16[32,384]{1,0:T(8,128)(2,1)S(1)}, f32[8,128]{1,0:T(8,128)S(1)}) custom-call(s32[1,1]{1,0:T(1,128)S(6)} %copy.15.count_ref, bf16[16,5,16,4,2,128]{5,4,3,2,1,0:T(2,128)(2,1)S(1)} %get-tuple-element.30.tiles_ref, bf16[5,16,2,128]{3,2,1,0:T(2,128)(2,1)S(1)} %collective-permute-done.edge_ref, ...), custom_call_target="tpu_custom_call" | custom-call | tf_op jit(solution)/shard_map/start/pallas_call | solution.py:464
  19.9 2.4 %collective-permute-start.4 = (bf16[32,384]{1,0:T(8,128)(2,1)S(1)}, bf16[32,384]{1,0:T(8,128)(2,1)S(1)}, u32[]{:S(2)}, u32[]{:S(2)}) collective-permute-start(bf16[32,384]{1,0:T(8,128)(2,1)S(1)} %get-tuple-element.40), channel_id=1, source_target_pairs={{0,24},{8,16},{16,8},{24,0},{1,25},{9,17},{17,9},{25,1},{2,26},{10... | collective-permute-start | bytes 73736 | tf_op jit(solution)/shard_map/ppermute | solution.py:50
  22.2 0.8 %collective-permute-start.3 = (bf16[32,384]{1,0:T(8,128)(2,1)S(1)}, bf16[32,384]{1,0:T(8,128)(2,1)S(1)}, u32[]{:S(2)}, u32[]{:S(2)}) collective-permute-start(bf16[32,384]{1,0:T(8,128)(2,1)S(1)} %get-tuple-element.40), channel_id=1, source_target_pairs={{0,8},{8,0},{16,24},{24,16},{1,9},{9,1},{17,25},{25,17},{2,10},{10... | collective-permute-start | bytes 73736 | tf_op jit(solution)/shard_map/ppermute | solution.py:50
  23.1 0.0 collective-permute-done.1.top_ref
  23.1 2.4 %outer.3 = (bf16[5,16,4,16,2,128]{5,4,3,2,1,0:T(2,128)(2,1)}, f32[8,128]{1,0:T(8,128)S(1)}) custom-call(bf16[16,5,16,4,2,128]{5,4,3,2,1,0:T(2,128)(2,1)S(1)} %get-tuple-element.30.tiles_ref, bf16[5,16,2,128]{3,2,1,0:T(2,128)(2,1)S(1)} %collective-permute-done.edge_ref, bf16[16,5,4,4,2,128]{5,4,3,2,1,0:T(2,128)(2,1)S(1)} %collective-permute-done.1.top_ref, ...), custom_call_target="tpu_custom_call" | custom-call | tf_op jit(solution)/shard_map/outer/pallas_call | solution.py:224
  25.4 0.1 collective-permute-done.4.two_ref
  25.5 0.5 collective-permute-done.3.one_ref
  26.1 3.0 %middle.2 = (f32[32,320]{1,0:T(8,128)S(1)}, f32[32,320]{1,0:T(8,128)S(1)}, bf16[32,384]{1,0:T(8,128)(2,1)S(1)}, f32[8,128]{1,0:T(8,128)S(1)}) custom-call(s32[1,1]{1,0:T(1,128)S(6)} %copy.15.count_ref, f32[32,320]{1,0:T(8,128)S(1)} %get-tuple-element.38.previous_ref.refs_3_, f32[8,128]{1,0:T(8,128)S(1)} %get-tuple-element.39.refs_0_.previous_exponent_ref, ...), custom_call_target="tpu_custom_call" | custom-call | tf_op jit(solution)/shard_map/middle/pallas_call | solution.py:487
  29.1 1.9 %collective-permute-start.6 = (bf16[32,384]{1,0:T(8,128)(2,1)S(1)}, bf16[32,384]{1,0:T(8,128)(2,1)S(1)}, u32[]{:S(2)}, u32[]{:S(2)}) collective-permute-start(bf16[32,384]{1,0:T(8,128)(2,1)S(1)} %get-tuple-element.46), channel_id=1, source_target_pairs={{0,24},{8,16},{16,8},{24,0},{1,25},{9,17},{17,9},{25,1},{2,26},{10... | collective-permute-start | bytes 73736 | tf_op jit(solution)/shard_map/ppermute | solution.py:50
  31.0 0.0 collective-permute-start.5
  31.0 3.2 %outer.4 = (bf16[5,16,4,16,2,128]{5,4,3,2,1,0:T(2,128)(2,1)}, f32[8,128]{1,0:T(8,128)S(1)}) custom-call(bf16[16,5,16,4,2,128]{5,4,3,2,1,0:T(2,128)(2,1)S(1)} %get-tuple-element.30.tiles_ref, bf16[5,16,2,128]{3,2,1,0:T(2,128)(2,1)S(1)} %collective-permute-done.edge_ref, ...), custom_call_target="tpu_custom_call", output_to_operand_aliasing={{0}: (5, {})} | custom-call | tf_op jit(solution)/shard_map/outer/pallas_call | solution.py:224
  34.1 0.7 %collective-permute-done.6.two_ref = bf16[32,384]{1,0:T(8,128)(2,1)S(1)} collective-permute-done((bf16[32,384]{1,0:T(8,128)(2,1)S(1)}, bf16[32,384]{1,0:T(8,128)(2,1)S(1)}, u32[]{:S(2)}, u32[]{:S(2)}) %collective-permute-start.6) | collective-permute-done | bytes 24608 | tf_op jit(solution)/shard_map/ppermute | solution.py:50
  34.8 0.7 %collective-permute-done.5.one_ref = bf16[32,384]{1,0:T(8,128)(2,1)S(1)} collective-permute-done((bf16[32,384]{1,0:T(8,128)(2,1)S(1)}, bf16[32,384]{1,0:T(8,128)(2,1)S(1)}, u32[]{:S(2)}, u32[]{:S(2)}) %collective-permute-start.5) | collective-permute-done | bytes 24608 | tf_op jit(solution)/shard_map/ppermute | solution.py:50
  35.5 3.0 %middle.3 = (f32[32,320]{1,0:T(8,128)S(1)}, f32[32,320]{1,0:T(8,128)S(1)}, bf16[32,384]{1,0:T(8,128)(2,1)S(1)}, f32[8,128]{1,0:T(8,128)S(1)}) custom-call(s32[1,1]{1,0:T(1,128)S(6)} %copy.15.count_ref, f32[32,320]{1,0:T(8,128)S(1)} %get-tuple-element.44.previous_ref.refs_4_, f32[8,128]{1,0:T(8,128)S(1)} %get-tuple-element.45.refs_0_.previous_exponent_ref.refs_1_, ...), custom_call_target="tpu_custom_call" | custom-call | tf_op jit(solution)/shard_map/middle/pallas_call | solution.py:487
  38.6 1.9 %collective-permute-start.8 = (bf16[32,384]{1,0:T(8,128)(2,1)S(1)}, bf16[32,384]{1,0:T(8,128)(2,1)S(1)}, u32[]{:S(2)}, u32[]{:S(2)}) collective-permute-start(bf16[32,384]{1,0:T(8,128)(2,1)S(1)} %get-tuple-element.54), channel_id=1, source_target_pairs={{0,24},{8,16},{16,8},{24,0},{1,25},{9,17},{17,9},{25,1},{2,26},{10... | collective-permute-start | bytes 73736 | tf_op jit(solution)/shard_map/ppermute | solution.py:50
  40.4 0.0 collective-permute-start.7
  40.4 3.2 %outer.5 = (bf16[5,16,4,16,2,128]{5,4,3,2,1,0:T(2,128)(2,1)}, f32[8,128]{1,0:T(8,128)S(1)}) custom-call(bf16[16,5,16,4,2,128]{5,4,3,2,1,0:T(2,128)(2,1)S(1)} %get-tuple-element.30.tiles_ref, bf16[5,16,2,128]{3,2,1,0:T(2,128)(2,1)S(1)} %collective-permute-done.edge_ref, ...), custom_call_target="tpu_custom_call", output_to_operand_aliasing={{0}: (5, {})} | custom-call | tf_op jit(solution)/shard_map/outer/pallas_call | solution.py:224
  43.6 0.6 %collective-permute-done.8.refs_4_ = bf16[32,384]{1,0:T(8,128)(2,1)S(1)} collective-permute-done((bf16[32,384]{1,0:T(8,128)(2,1)S(1)}, bf16[32,384]{1,0:T(8,128)(2,1)S(1)}, u32[]{:S(2)}, u32[]{:S(2)}) %collective-permute-start.8) | collective-permute-done | bytes 24608 | tf_op jit(solution)/shard_map/ppermute | solution.py:50
  44.3 0.2 collective-permute-done.7.refs_3_
  44.5 0.4 gram.1
  45.0 9.2 %all_to_all.5.parts_ref = f32[32,1,128]{2,1,0:T(1,128)S(1)} all-to-all(f32[32,1,128]{2,1,0:T(1,128)S(1)} %gram.1), channel_id=1, replica_groups=mesh['gx'=4,'gy'=8] {'gx','gy'}, dimensions={0} | all-to-all | bytes 32768 | tf_op jit(solution)/shard_map/all_to_all | solution.py:508
  54.1 1.5 %finish.1 = f32[32,320]{1,0:T(8,128)} custom-call(f32[32,1,128]{2,1,0:T(1,128)S(1)} %all_to_all.5.parts_ref, f32[8,128]{1,0:T(8,128)S(1)} %get-tuple-element.39.refs_0_.previous_exponent_ref, f32[8,128]{1,0:T(8,128)S(1)} %get-tuple-element.45.refs_0_.previous_exponent_ref.refs_1_, f32[8,128]{1,0:T(8,128)S(1)} %get-tuple-element.49.refs_0_.refs_2_, ...), custom_call_target="tpu_custom_call" | custom-call | tf_op jit(solution)/shard_map/finish/pallas_call | solution.py:509
Async XLA Ops:
  2.4 20.7 %collective-permute-start.1 = (bf16[16,5,4,4,2,128]{5,4,3,2,1,0:T(2,128)(2,1)S(1)}, bf16[16,5,4,4,2,128]{5,4,3,2,1,0:T(2,128)(2,1)S(1)}, u32[]{:S(2)}, u32[]{:S(2)}) collective-permute-start(bf16[16,5,4,4,2,128]{5,4,3,2,1,0:T(2,128)(2,1)S(1)} %get-tuple-element.32), channel_id=1, source_target_pairs={{0,1},{1,2},{2,3},{3,4},{4,5},{5,6},{6,7},{8,9},{9,10},{10,11},{11... | collective-permute-start | bytes 1966088 | tf_op jit(solution)/shard_map/ppermute | solution.py:41
  4.9 11.2 %collective-permute-start = (bf16[5,16,2,128]{3,2,1,0:T(2,128)(2,1)S(1)}, bf16[5,16,2,128]{3,2,1,0:T(2,128)(2,1)S(1)}, u32[]{:S(2)}, u32[]{:S(2)}) collective-permute-start(bf16[5,16,2,128]{3,2,1,0:T(2,128)(2,1)S(1)} %get-tuple-element.31), channel_id=1, source_target_pairs={{0,8},{8,16},{16,24},{24,0},{1,9},{9,17},{17,25},{25,1},{2,10},{10... | collective-permute-start | bytes 122888 | tf_op jit(solution)/shard_map/ppermute | solution.py:427
  7.3 8.8 %collective-permute-start.2 = (bf16[5,4,4,2,128]{4,3,2,1,0:T(2,128)(2,1)S(1)}, bf16[5,4,4,2,128]{4,3,2,1,0:T(2,128)(2,1)S(1)}, u32[]{:S(2)}, u32[]{:S(2)}) collective-permute-start(bf16[5,4,4,2,128]{4,3,2,1,0:T(2,128)(2,1)S(1)} %get-tuple-element.34), channel_id=1, source_target_pairs={{0,1},{1,2},{2,3},{3,4},{4,5},{5,6},{6,7},{8,9},{9,10},{10,11},{11... | collective-permute-start | bytes 122888 | tf_op jit(solution)/shard_map/ppermute | solution.py:41
  19.9 5.7 %collective-permute-start.4 = (bf16[32,384]{1,0:T(8,128)(2,1)S(1)}, bf16[32,384]{1,0:T(8,128)(2,1)S(1)}, u32[]{:S(2)}, u32[]{:S(2)}) collective-permute-start(bf16[32,384]{1,0:T(8,128)(2,1)S(1)} %get-tuple-element.40), channel_id=1, source_target_pairs={{0,24},{8,16},{16,8},{24,0},{1,25},{9,17},{17,9},{25,1},{2,26},{10... | collective-permute-start | bytes 73736 | tf_op jit(solution)/shard_map/ppermute | solution.py:50
  22.2 3.8 %collective-permute-start.3 = (bf16[32,384]{1,0:T(8,128)(2,1)S(1)}, bf16[32,384]{1,0:T(8,128)(2,1)S(1)}, u32[]{:S(2)}, u32[]{:S(2)}) collective-permute-start(bf16[32,384]{1,0:T(8,128)(2,1)S(1)} %get-tuple-element.40), channel_id=1, source_target_pairs={{0,8},{8,0},{16,24},{24,16},{1,9},{9,1},{17,25},{25,17},{2,10},{10... | collective-permute-start | bytes 73736 | tf_op jit(solution)/shard_map/ppermute | solution.py:50
  29.1 5.7 %collective-permute-start.6 = (bf16[32,384]{1,0:T(8,128)(2,1)S(1)}, bf16[32,384]{1,0:T(8,128)(2,1)S(1)}, u32[]{:S(2)}, u32[]{:S(2)}) collective-permute-start(bf16[32,384]{1,0:T(8,128)(2,1)S(1)} %get-tuple-element.46), channel_id=1, source_target_pairs={{0,24},{8,16},{16,8},{24,0},{1,25},{9,17},{17,9},{25,1},{2,26},{10... | collective-permute-start | bytes 73736 | tf_op jit(solution)/shard_map/ppermute | solution.py:50
  31.0 4.6 %collective-permute-start.5 = (bf16[32,384]{1,0:T(8,128)(2,1)S(1)}, bf16[32,384]{1,0:T(8,128)(2,1)S(1)}, u32[]{:S(2)}, u32[]{:S(2)}) collective-permute-start(bf16[32,384]{1,0:T(8,128)(2,1)S(1)} %get-tuple-element.46), channel_id=1, source_target_pairs={{0,8},{8,0},{16,24},{24,16},{1,9},{9,1},{17,25},{25,17},{2,10},{10... | collective-permute-start | bytes 73736 | tf_op jit(solution)/shard_map/ppermute | solution.py:50
  38.6 5.7 %collective-permute-start.8 = (bf16[32,384]{1,0:T(8,128)(2,1)S(1)}, bf16[32,384]{1,0:T(8,128)(2,1)S(1)}, u32[]{:S(2)}, u32[]{:S(2)}) collective-permute-start(bf16[32,384]{1,0:T(8,128)(2,1)S(1)} %get-tuple-element.54), channel_id=1, source_target_pairs={{0,24},{8,16},{16,8},{24,0},{1,25},{9,17},{17,9},{25,1},{2,26},{10... | collective-permute-start | bytes 73736 | tf_op jit(solution)/shard_map/ppermute | solution.py:50
  40.4 4.1 %collective-permute-start.7 = (bf16[32,384]{1,0:T(8,128)(2,1)S(1)}, bf16[32,384]{1,0:T(8,128)(2,1)S(1)}, u32[]{:S(2)}, u32[]{:S(2)}) collective-permute-start(bf16[32,384]{1,0:T(8,128)(2,1)S(1)} %get-tuple-element.54), channel_id=1, source_target_pairs={{0,8},{8,0},{16,24},{24,16},{1,9},{9,1},{17,25},{25,17},{2,10},{10... | collective-permute-start | bytes 73736 | tf_op jit(solution)/shard_map/ppermute | solution.py:50

commit v2 on v1

--- a/solution.py
+++ b/solution.py
@@ -6,6 +6,7 @@
 from jax.experimental.pallas import tpu as pltpu
 from jax.sharding import PartitionSpec as P
 
+
 Q = 4
 ITERS = 3
 
@@ -17,13 +18,14 @@
 
 LANES = 128
 GROUP = 8
+PRICE = 16 << 20
 VMEM_BYTES = 24 << 20
 bf16 = jnp.bfloat16
 f32 = jnp.float32
 
 in_vmem = pl.BlockSpec(memory_space=pltpu.VMEM)
+in_smem = pl.BlockSpec(memory_space=pltpu.SMEM)
 in_hbm = pl.BlockSpec(memory_space=pltpu.HBM)
-in_smem = pl.BlockSpec(memory_space=pltpu.SMEM)
 params = pltpu.CompilerParams(vmem_limit_bytes=VMEM_BYTES)
 
 
@@ -34,11 +36,6 @@
 def ring(axis, by):
     count = lax.axis_size(axis)
     return [(i, (i + by) % count) for i in range(count)]
-
-
-def from_below(array, axis):
-    count = lax.axis_size(axis)
-    return lax.ppermute(array, axis, [(i, i + 1) for i in range(count - 1)])
 
 
 def neighbours(array, axis):
@@ -80,47 +77,39 @@
     return jnp.swapaxes(array, -3, -2).reshape(*lead, rows, tiles * lanes)
 
 
-def faces_kernel(state_ref, edge_ref, corner_ref, top_ref, sem):
-    comps, _, _, tiles, rows, lanes = state_ref.shape
-    top = [
-        pltpu.make_async_copy(
-            state_ref.at[:, pl.ds(k * Q + Q - 1, 1), :, t], top_ref.at[t, :, pl.ds(k, 1)], sem.at[2 + Q + t * Q + k]
-        )
-        for t in range(tiles)
+def top_row(state_ref, t, k, target_ref, sem):
+    return pltpu.make_async_copy(state_ref.at[:, pl.ds(k * Q + Q - 1, 1), :, t], target_ref.at[:, pl.ds(k, 1)], sem)
+
+
+def faces_kernel(state_ref, edge_ref, corner_ref, sem):
+    tiles = state_ref.shape[3]
+    copies = [top_row(state_ref, 0, k, corner_ref, sem.at[k]) for k in range(Q)]
+    copies.append(pltpu.make_async_copy(state_ref.at[:, :, Q - 1, tiles - 1], edge_ref, sem.at[Q]))
+    for copy in copies:
+        copy.start()
+    for copy in copies:
+        copy.wait()
+
+
+def prep_kernel(
+    state_ref, rhs_ref, sigma_ref, deriv_ref, stiff_ref, expand_ref, jump_ref,
+    top_ref, tile_ref, rhs_out_ref, sigma_out_ref, full_ref, first_ref, block_ref,
+    deriv_in, stiff_in, expand_in, jump_in, sem,
+):
+    count = top_ref.shape[0]
+    pairs_of_refs = [
+        (deriv_ref, deriv_in), (expand_ref, expand_in), (jump_ref, jump_in), (stiff_ref, stiff_in),
+        (state_ref.at[:, :, :, 0], tile_ref), (rhs_ref, rhs_out_ref), (sigma_ref, sigma_out_ref),
+    ]
+    copies = [pltpu.make_async_copy(a, b, sem.at[at]) for at, (a, b) in enumerate(pairs_of_refs)]
+    copies += [
+        top_row(state_ref, t, k, top_ref.at[t], sem.at[len(pairs_of_refs) + t * Q + k])
+        for t in range(count)
         for k in range(Q)
     ]
-    copies = [pltpu.make_async_copy(state_ref.at[:, :, Q - 1, tiles - 1], edge_ref, sem.at[0])]
-    copies += [
-        pltpu.make_async_copy(
-            state_ref.at[:, pl.ds(k * Q + Q - 1, 1), :, 0], corner_ref.at[:, pl.ds(k, 1)], sem.at[1 + k]
-        )
-        for k in range(Q)
-    ]
-    for copy in copies + top:
+    for copy in copies:
         copy.start()
-    for copy in copies + top:
-        copy.wait()
-
-
-def prep_kernel(
-    state_ref, blocks_ref, rhs_ref, sigma_ref, deriv_ref, stiff_ref, expand_ref, jump_ref,
-    tiles_ref, blocks_out_ref, rhs_out_ref, sigma_out_ref, full_ref, first_ref, block_ref,
-    deriv_in, stiff_in, expand_in, jump_in, sem,
-):
-    count = tiles_ref.shape[0]
-    small = [
-        pltpu.make_async_copy(source, target, sem.at[at])
-        for at, (source, target) in enumerate([
-            (deriv_ref, deriv_in), (expand_ref, expand_in), (jump_ref, jump_in), (stiff_ref, stiff_in),
-            (rhs_ref, rhs_out_ref), (sigma_ref, sigma_out_ref), (blocks_ref, blocks_out_ref),
-        ])
-    ]
-    large = [
-        pltpu.make_async_copy(state_ref.at[:, :, :, t], tiles_ref.at[t], sem.at[len(small) + t]) for t in range(count)
-    ]
-    for copy in small[:-1] + large + small[-1:]:
-        copy.start()
-    for copy in small[:4]:
+    for copy in copies[:4]:
         copy.wait()
     size, nodes = expand_in.shape
     rows = size // nodes
@@ -135,15 +124,18 @@
         both = jnp.dot(expand, wide, preferred_element_type=f32)
         full_ref[:, d * size : (d + 1) * size] = jnp.where(same, both, 0.0).astype(bf16)
         first_ref[:, d * size : (d + 1) * size] = jnp.where(own, wide.astype(f32), 0.0).astype(bf16)
-    full_ref[:, 3 * size :] = jump_in[:size]
-    first_ref[:, 3 * size :] = jump_in[size:]
+    jump = jump_in[...]
+    below = lax.broadcasted_iota(jnp.int32, jump.shape, 1) >= jump.shape[1] - size // Q
+    jump = jnp.where(below & (lax.axis_index("gy") == 0), 0.0, jump.astype(f32)).astype(bf16)
+    full_ref[:, 3 * size :] = jump[:size]
+    first_ref[:, 3 * size :] = jump[size:]
     block_ref[...] = jnp.zeros_like(block_ref)
     high, low = split(stiff_in[...])
     for v in range(block_ref.shape[1] // nodes):
         at = slice(v * nodes, (v + 1) * nodes)
         block_ref[0, at, at] = high
         block_ref[1, at, at] = low
-    for copy in small[4:-1] + large + small[-1:]:
+    for copy in copies[4:]:
         copy.wait()
 
 
@@ -253,24 +245,27 @@
     return value * jnp.exp2(-by), by
 
 
-def apply_blocks(count, value_ref, blocks_ref, out_ref):
+def group_count(count):
+    return (count + GROUP - 1) // GROUP
+
+
+def apply_blocks(count, value_ref, block_at, out_ref):
     _, order = value_ref.shape
     rows = lax.broadcasted_iota(jnp.int32, (2 * GROUP, order), 0)
     out_ref[...] = jnp.zeros_like(out_ref)
 
     def group(g, carry):
         base = pl.multiple_of(g * GROUP, GROUP)
+        block = block_at(g)
         terms = jnp.concatenate(split(value_ref[pl.ds(base, GROUP), :]), axis=0)
         kept = jnp.zeros((2 * GROUP, order), f32)
         for s in range(GROUP):
-            product = lax.dot_general(
-                terms, blocks_ref[base + s], (((1,), (1,)), ((), ())), preferred_element_type=f32
-            )
+            product = jnp.dot(terms, block(base + s), preferred_element_type=f32)
             kept = jnp.where((rows == s) | (rows == s + GROUP), product, kept)
         out_ref[pl.ds(base, GROUP), :] = kept[:GROUP] + kept[GROUP:]
         return carry
 
-    lax.fori_loop(0, (count + GROUP - 1) // GROUP, group, 0)
+    lax.fori_loop(0, group_count(count), group, 0)
 
 
 def emit(direction_ref, exponent, sent_ref, exponent_ref):
@@ -285,17 +280,41 @@
 
 
 def start_kernel(
-    count_ref, tiles_ref, edge_ref, corner_ref, first_ref, rhs_ref, blocks_ref,
-    basis_ref, direction_ref, sent_ref, exponent_ref, stack_ref, speed_ref, trace_ref,
+    count_ref, state_ref, blocks_in_ref, tile_ref, edge_ref, corner_ref, first_ref, rhs_ref,
+    basis_ref, direction_ref, sent_ref, exponent_ref, tiles_ref, blocks_ref,
+    stack_ref, speed_ref, trace_ref, stage_ref, tile_sem, block_sem,
 ):
     slots, order = rhs_ref.shape
-    _, comps, faces, _, rows, _ = tiles_ref.shape
+    tiles, comps, faces, _, rows, _ = tiles_ref.shape
+    count = count_ref[0, 0]
+
+    def tile_copy(t):
+        return pltpu.make_async_copy(state_ref.at[:, :, :, t], tiles_ref.at[t], tile_sem.at[t])
+
+    def block_copy(g):
+        part = pl.ds(g * GROUP, GROUP)
+        return pltpu.make_async_copy(blocks_in_ref.at[part], stage_ref.at[part], block_sem.at[g])
+
+    def arrived(g):
+        block_copy(g).wait()
+
+        def block(at):
+            turned = stage_ref[at].T
+            blocks_ref[at] = turned
+            return turned
+
+        return block
+
+    for g in range(slots // GROUP):
+        pl.when(g < group_count(count))(block_copy(g).start)
+    for t in range(tiles):
+        tile_copy(t).start()
     nodes = order // comps
     size, face = nodes * rows, faces * rows
     columns = fill_columns(
         stack_ref, speed_ref,
-        lambda v: tiles_ref[0, v].reshape(size, LANES),
-        lambda v: tiles_ref[0, v, :, Q - 1].reshape(face, LANES),
+        lambda v: tile_ref[v].reshape(size, LANES),
+        lambda v: tile_ref[v, :, Q - 1].reshape(face, LANES),
         lambda v: edge_ref[v].reshape(face, LANES),
         lambda v: corner_ref[v].reshape(face, LANES),
         comps,
@@ -303,12 +322,13 @@
     for v in columns:
         value = jnp.dot(first_ref[...], stack_ref[...], preferred_element_type=f32)
         trace_ref[:, v * nodes : (v + 1) * nodes] = value.T[:slots]
-    count = count_ref[0, 0]
     rhs = live_rows(count, rhs_ref.shape) * (rhs_ref[...] + time_step * trace_ref[...])
     basis, exponent = rescale(rhs)
     basis_ref[...] = basis
-    apply_blocks(count, basis_ref, blocks_ref, direction_ref)
+    apply_blocks(count, basis_ref, arrived, direction_ref)
     emit(direction_ref, exponent, sent_ref, exponent_ref)
+    for t in range(tiles):
+        tile_copy(t).wait()
 
 
 def operate(count_ref, direction_ref, exponent_ref, one_ref, two_ref, sigma_ref, stiff_ref):
@@ -337,7 +357,7 @@
         count_ref, previous_ref, previous_exponent_ref, one_ref, two_ref, sigma_ref, stiff_ref
     )
     basis_ref[...] = basis
-    apply_blocks(count_ref[0, 0], basis_ref, blocks_ref, direction_ref)
+    apply_blocks(count_ref[0, 0], basis_ref, lambda g: lambda at: blocks_ref[at], direction_ref)
     emit(direction_ref, exponent, sent_ref, exponent_ref)
 
 
@@ -405,45 +425,45 @@
     out_ref[...] = total
 
 
-def per_device(outer_state, derivative, stiffness, wall_rhs, wall_sigma, wall_inverse, wall_count):
+def solve(outer_state, derivative, stiffness, wall_rhs, wall_sigma, wall_inverse, wall_count):
     comps, nodes, rows, cols = outer_state.shape
     slots, order = wall_rhs.shape
     faces = nodes // Q
     size = nodes * rows
     state = held_in_hbm(tile_view(outer_state.reshape(comps, faces, Q, rows, cols)))
     count = cols // LANES
-    edge_shape = jax.ShapeDtypeStruct((comps, faces, rows, LANES), bf16)
-    corner_shape = jax.ShapeDtypeStruct((comps, Q, Q, rows, LANES), bf16)
-
-    edge, corner, top = pl.pallas_call(
+    edge, corner = pl.pallas_call(
         faces_kernel,
         in_specs=[in_hbm],
-        out_specs=[in_vmem] * 3,
-        out_shape=[edge_shape, corner_shape, jax.ShapeDtypeStruct((count, *corner_shape.shape), bf16)],
-        scratch_shapes=[pltpu.SemaphoreType.DMA((2 + Q + count * Q,))],
+        out_specs=[in_vmem] * 2,
+        out_shape=[
+            jax.ShapeDtypeStruct((comps, faces, rows, LANES), bf16),
+            jax.ShapeDtypeStruct((comps, Q, Q, rows, LANES), bf16),
+        ],
+        scratch_shapes=[pltpu.SemaphoreType.DMA((Q + 1,))],
         compiler_params=params,
+        cost_estimate=pl.CostEstimate(flops=0, transcendentals=0, bytes_accessed=PRICE),
         name="faces",
     )(state)
+    came_corner = lax.ppermute(corner, "gy", ring("gy", 1))
     came_edge = lax.ppermute(edge, "gx", ring("gx", 1))
-    came_corner = from_below(corner, "gy")
-    came_top = from_below(top, "gy")
 
     jumps = jump_matrix(nodes, rows)
     depth = 3 * size + jumps.shape[1]
     expand = np.repeat(np.eye(nodes, dtype=np.float32), rows, axis=0)
     jumps = np.concatenate([jumps, jumps[::rows]])
     operands = (
-        state, wall_inverse, wall_rhs, wall_sigma, derivative, stiffness, jnp.asarray(expand, bf16),
+        state, wall_rhs, wall_sigma, derivative, stiffness, jnp.asarray(expand, bf16),
         jnp.asarray(jumps, bf16),
     )
     operands = tuple(held_in_hbm(operand) for operand in operands)
-    tiles, blocks, rhs, sigma, full, first, stiff = pl.pallas_call(
+    top, tile, rhs, sigma, full, first, stiff = pl.pallas_call(
         prep_kernel,
         in_specs=[in_hbm] * len(operands),
         out_specs=[in_vmem] * 7,
         out_shape=[
-            jax.ShapeDtypeStruct((count, comps, faces, Q, rows, LANES), bf16),
-            jax.ShapeDtypeStruct(wall_inverse.shape, bf16),
+            jax.ShapeDtypeStruct((count, *corner.shape), bf16),
+            jax.ShapeDtypeStruct((comps, faces, Q, rows, LANES), bf16),
             jax.ShapeDtypeStruct(wall_rhs.shape, f32),
             jax.ShapeDtypeStruct(wall_sigma.shape, f32),
             jax.ShapeDtypeStruct((size, depth), bf16),
@@ -451,27 +471,35 @@
             jax.ShapeDtypeStruct((2, order, order), bf16),
         ],
         scratch_shapes=[pltpu.VMEM(a.shape, a.dtype) for a in (derivative, stiffness)]
-        + [pltpu.VMEM(expand.shape, bf16), pltpu.VMEM(jumps.shape, bf16), pltpu.SemaphoreType.DMA((7 + count,))],
+        + [pltpu.VMEM(expand.shape, bf16), pltpu.VMEM(jumps.shape, bf16)]
+        + [pltpu.SemaphoreType.DMA((7 + count * Q,))],
         compiler_params=params,
+        cost_estimate=pl.CostEstimate(flops=0, transcendentals=0, bytes_accessed=PRICE),
         name="prep",
     )(*operands)
+    came_top = lax.ppermute(top, "gy", ring("gy", 1))
 
     vector = jax.ShapeDtypeStruct((slots, order), f32)
     padded = -(-(order + 1) // LANES) * LANES
     step_shapes = [
         vector, vector, jax.ShapeDtypeStruct((slots, padded), bf16), jax.ShapeDtypeStruct((8, LANES), f32),
     ]
-    basis, direction, sent, exponent = pl.pallas_call(
+    basis, direction, sent, exponent, tiles, blocks = pl.pallas_call(
         start_kernel,
-        in_specs=[in_smem] + [in_vmem] * 6,
-        out_specs=[in_vmem] * 4,
-        out_shape=step_shapes,
+        in_specs=[in_smem] + [in_hbm] * 2 + [in_vmem] * 5,
+        out_specs=[in_vmem] * 6,
+        out_shape=step_shapes + [
+            jax.ShapeDtypeStruct((count, comps, faces, Q, rows, LANES), bf16),
+            jax.ShapeDtypeStruct(wall_inverse.shape, bf16),
+        ],
         scratch_shapes=[
             pltpu.VMEM((depth, LANES), bf16), pltpu.VMEM((3, size, LANES), f32), pltpu.VMEM((slots, order), f32),
+            pltpu.VMEM(wall_inverse.shape, bf16),
+            pltpu.SemaphoreType.DMA((count,)), pltpu.SemaphoreType.DMA((slots // GROUP,)),
         ],
         compiler_params=params,
         name="start",
-    )(wall_count, tiles, came_edge, came_corner, first, rhs, blocks)
+    )(wall_count, state, held_in_hbm(wall_inverse), tile, came_edge, came_corner, first, rhs)
     bases, directions, exponents = [basis], [direction], [exponent]
 
     width = 2 * LANES
@@ -528,6 +556,4 @@
         P("gx", "gy"),
     )
     out_specs = (P(None, None, "gy", "gx"), P(("gx", "gy"), None))
-    return jax.shard_map(
-        per_device, mesh=mesh, in_specs=in_specs, out_specs=out_specs, check_vma=False
-    )
+    return jax.shard_map(solve, mesh=mesh, in_specs=in_specs, out_specs=out_specs, check_vma=False)

time: 55.9 us -> 56.8 us (1.016)
  waiting for transfers between devices: 2.91 us -> 8.24 us
  Pallas kernels: 27 us -> 24.1 us
  starting transfers between devices: 15.2 us -> 13.5 us
    ppermute x3, waiting for transfers between devices: 0.01 us -> 6.09 us  [the longest x1 4.04 us: solve(): came_corner = lax.ppermute(corner, 'gy', ring('gy', 1))]
    ppermute x3, starting transfers between devices: 8.23 us -> 4.48 us  [the longest x1 2.64 us: solve(): came_edge = lax.ppermute(edge, 'gx', ring('gx', 1))]
    pallas_call x7, Pallas kernels: 18.2 us -> 15.2 us  [the longest x1 6.19 us: solve(): pl.pallas_call(start_kernel, in_specs=[in_smem] + [in_hbm] * 2 + [in_vmem...]
    ppermute x6, starting transfers between devices: 6.97 us -> 8.99 us  [neighbours(): return (lax.ppermute(array, axis, even), lax.ppermute(array, axis, odd))]
    ppermute x6, waiting for transfers between devices: 2.9 us -> 2.15 us  [neighbours(): return (lax.ppermute(array, axis, even), lax.ppermute(array, axis, odd))]
  transfers between devices with their start and end apart: 9 -> 9, of which waited for: 6 -> 6; matrix products, arithmetic and copies ran while one was open for 0% -> 0% of each run, Pallas kernels for 31% -> 28%
where the time goes in v2:
time: 56.8 us; the launch traced here: 56.6 us
  Pallas kernels  24.1 us (42%)
  starting transfers between devices  13.5 us (24%)
  blocking collectives  9.38 us (17%)
  waiting for transfers between devices  8.24 us (15%)
  between operations  1.38 us (2%)
    all_to_all x1, blocking collectives, solve(): parts = lax.all_to_all(part, ('gx', 'gy'), 0, 0)  9.38 us
    ppermute x6, starting transfers between devices, neighbours(): return (lax.ppermute(array, axis, even), lax.ppermute(array, axis, odd))  8.99 us
    pallas_call x3, Pallas kernels, outer_piece(): pl.pallas_call(kernel, in_specs=specs, out_specs=[in_hbm, in_vmem], out_s...  8.98 us
    pallas_call x1, Pallas kernels, solve(): pl.pallas_call(start_kernel, in_specs=[in_smem] + [in_hbm] * 2 + [in_vmem...  6.19 us
    ppermute x1, waiting for transfers between devices, solve(): came_corner = lax.ppermute(corner, 'gy', ring('gy', 1))  4.04 us
    pallas_call x2, Pallas kernels, solve(): pl.pallas_call(middle_kernel, in_specs=[in_smem] + [in_vmem] * 8, out_spe...  3.84 us
    ppermute x1, starting transfers between devices, solve(): came_edge = lax.ppermute(edge, 'gx', ring('gx', 1))  2.64 us
    pallas_call x1, Pallas kernels, solve(): pl.pallas_call(prep_kernel, in_specs=[in_hbm] * len(operands), out_specs=...  2.3 us
  transfers between devices with their start and end apart: 9, of which 6 were waited for; matrix products, arithmetic and copies ran while one was open for 0% of the time, Pallas kernels for 28%

profile of v2, /device:TPU:0, one launch (start us, length us, event | category | flops | bytes accessed | tf_op | source)
XLA Modules:
  0.0 56.6 jit_solution(10010344413588902556)
XLA Ops:
  0.6 2.3 %prep.1 = (bf16[16,5,4,4,2,128]{5,4,3,2,1,0:T(2,128)(2,1)S(1)}, bf16[5,16,4,2,128]{4,3,2,1,0:T(2,128)(2,1)S(1)}, f32[32,320]{1,0:T(8,128)S(1)}, f32[32,320]{1,0:...) custom-call(bf16[5,16,4,16,2,128]{5,4,3,2,1,0:T(2,128)(2,1)} %bitcast.6, ...), custom_call_target="tpu_custom_call" | custom-call | bytes 16777216 | tf_op jit(solution)/shard_map/prep/pallas_call | solution.py:460
  2.9 0.5 collective-permute-start.2
  3.5 0.9 %faces.1 = (bf16[5,16,2,128]{3,2,1,0:T(2,128)(2,1)S(1)}, bf16[5,4,4,2,128]{4,3,2,1,0:T(2,128)(2,1)S(1)}) custom-call(bf16[5,16,4,16,2,128]{5,4,3,2,1,0:T(2,128)(2,1)} %bitcast.7), custom_call_target="tpu_custom_call" | custom-call | bytes 16777216 | tf_op jit(solution)/shard_map/faces/pallas_call | solution.py:435
  4.4 2.6 %collective-permute-start = (bf16[5,16,2,128]{3,2,1,0:T(2,128)(2,1)S(1)}, bf16[5,16,2,128]{3,2,1,0:T(2,128)(2,1)S(1)}, u32[]{:S(2)}, u32[]{:S(2)}) collective-permute-start(bf16[5,16,2,128]{3,2,1,0:T(2,128)(2,1)S(1)} %get-tuple-element.32), channel_id=1, source_target_pairs={{0,8},{8,16},{16,24},{24,0},{1,9},{9,17},{17,25},{25,1},{2,10},{10... | collective-permute-start | bytes 122888 | tf_op jit(solution)/shard_map/ppermute | solution.py:449
  7.0 1.3 %collective-permute-start.1 = (bf16[5,4,4,2,128]{4,3,2,1,0:T(2,128)(2,1)S(1)}, bf16[5,4,4,2,128]{4,3,2,1,0:T(2,128)(2,1)S(1)}, u32[]{:S(2)}, u32[]{:S(2)}) collective-permute-start(bf16[5,4,4,2,128]{4,3,2,1,0:T(2,128)(2,1)S(1)} %get-tuple-element.33), channel_id=1, source_target_pairs={{0,1},{1,2},{2,3},{3,4},{4,5},{5,6},{6,7},{7,0},{8,9},{9,10},{10,1... | collective-permute-start | bytes 122888 | tf_op jit(solution)/shard_map/ppermute | solution.py:448
  9.0 2.1 %collective-permute-done.edge_ref = bf16[5,16,2,128]{3,2,1,0:T(2,128)(2,1)S(1)} collective-permute-done((bf16[5,16,2,128]{3,2,1,0:T(2,128)(2,1)S(1)}, bf16[5,16,2,128]{3,2,1,0:T(2,128)(2,1)S(1)}, u32[]{:S(2)}, u32[]{:S(2)}) %collective-permute-start) | collective-permute-done | bytes 40992 | tf_op jit(solution)/shard_map/ppermute | solution.py:449
  11.0 4.0 %collective-permute-done.1.corner_ref = bf16[5,4,4,2,128]{4,3,2,1,0:T(2,128)(2,1)S(1)} collective-permute-done((bf16[5,4,4,2,128]{4,3,2,1,0:T(2,128)(2,1)S(1)}, bf16[5,4,4,2,128]{4,3,2,1,0:T(2,128)(2,1)S(1)}, u32[]{:S(2)}, u32[]{:S(2)}) %collective-permute-start.1) | collective-permute-done | bytes 40992 | tf_op jit(solution)/shard_map/ppermute | solution.py:448
  15.1 6.2 %start.1 = (f32[32,320]{1,0:T(8,128)S(1)}, f32[32,320]{1,0:T(8,128)S(1)}, bf16[32,384]{1,0:T(8,128)(2,1)S(1)}, f32[8,128]{1,0:T(8,128)S(1)}, bf16[16,5,16,4,2,12...) custom-call(s32[1,1]{1,0:T(1,128)S(6)} %copy.15.count_ref, bf16[5,16,4,16,2,128]{5,4,3,2,1,0:T(2,128)(2,1)} %bitcast.8, ...), custom_call_target="tpu_custom_call" | custom-call | tf_op jit(solution)/shard_map/start/pallas_call | solution.py:487
  21.3 4.4 %collective-permute-start.4 = (bf16[32,384]{1,0:T(8,128)(2,1)S(1)}, bf16[32,384]{1,0:T(8,128)(2,1)S(1)}, u32[]{:S(2)}, u32[]{:S(2)}) collective-permute-start(bf16[32,384]{1,0:T(8,128)(2,1)S(1)} %get-tuple-element.41), channel_id=1, source_target_pairs={{0,24},{8,16},{16,8},{24,0},{1,25},{9,17},{17,9},{25,1},{2,26},{10... | collective-permute-start | bytes 73736 | tf_op jit(solution)/shard_map/ppermute | solution.py:47
  25.7 0.0 collective-permute-start.3
  25.7 0.0 collective-permute-done.2.top_ref
  25.7 2.4 %outer.3 = (bf16[5,16,4,16,2,128]{5,4,3,2,1,0:T(2,128)(2,1)}, f32[8,128]{1,0:T(8,128)S(1)}) custom-call(bf16[16,5,16,4,2,128]{5,4,3,2,1,0:T(2,128)(2,1)S(1)} %get-tuple-element.36.tiles_ref, bf16[5,16,2,128]{3,2,1,0:T(2,128)(2,1)S(1)} %collective-permute-done.edge_ref, bf16[16,5,4,4,2,128]{5,4,3,2,1,0:T(2,128)(2,1)S(1)} %collective-permute-done.2.top_ref, ...), custom_call_target="tpu_custom_call" | custom-call | tf_op jit(solution)/shard_map/outer/pallas_call | solution.py:216
  28.1 0.0 collective-permute-done.4.two_ref
  28.1 1.4 %collective-permute-done.3.one_ref = bf16[32,384]{1,0:T(8,128)(2,1)S(1)} collective-permute-done((bf16[32,384]{1,0:T(8,128)(2,1)S(1)}, bf16[32,384]{1,0:T(8,128)(2,1)S(1)}, u32[]{:S(2)}, u32[]{:S(2)}) %collective-permute-start.3) | collective-permute-done | bytes 24608 | tf_op jit(solution)/shard_map/ppermute | solution.py:47
  29.5 1.9 %middle.2 = (f32[32,320]{1,0:T(8,128)S(1)}, f32[32,320]{1,0:T(8,128)S(1)}, bf16[32,384]{1,0:T(8,128)(2,1)S(1)}, f32[8,128]{1,0:T(8,128)S(1)}) custom-call(s32[1,1]{1,0:T(1,128)S(6)} %copy.15.count_ref, f32[32,320]{1,0:T(8,128)S(1)} %get-tuple-element.39.previous_ref.refs_3_, f32[8,128]{1,0:T(8,128)S(1)} %get-tuple-element.40.refs_0_.previous_exponent_ref, ...), custom_call_target="tpu_custom_call" | custom-call | tf_op jit(solution)/shard_map/middle/pallas_call | solution.py:515
  31.4 2.1 %collective-permute-start.6 = (bf16[32,384]{1,0:T(8,128)(2,1)S(1)}, bf16[32,384]{1,0:T(8,128)(2,1)S(1)}, u32[]{:S(2)}, u32[]{:S(2)}) collective-permute-start(bf16[32,384]{1,0:T(8,128)(2,1)S(1)} %get-tuple-element.48), channel_id=1, source_target_pairs={{0,24},{8,16},{16,8},{24,0},{1,25},{9,17},{17,9},{25,1},{2,26},{10... | collective-permute-start | bytes 73736 | tf_op jit(solution)/shard_map/ppermute | solution.py:47
  33.6 0.0 collective-permute-start.5
  33.6 3.3 %outer.4 = (bf16[5,16,4,16,2,128]{5,4,3,2,1,0:T(2,128)(2,1)}, f32[8,128]{1,0:T(8,128)S(1)}) custom-call(bf16[16,5,16,4,2,128]{5,4,3,2,1,0:T(2,128)(2,1)S(1)} %get-tuple-element.36.tiles_ref, bf16[5,16,2,128]{3,2,1,0:T(2,128)(2,1)S(1)} %collective-permute-done.edge_ref, ...), custom_call_target="tpu_custom_call", output_to_operand_aliasing={{0}: (5, {})} | custom-call | tf_op jit(solution)/shard_map/outer/pallas_call | solution.py:216
  36.8 0.3 collective-permute-done.6.two_ref
  37.1 0.3 collective-permute-done.5.one_ref
  37.4 1.9 %middle.3 = (f32[32,320]{1,0:T(8,128)S(1)}, f32[32,320]{1,0:T(8,128)S(1)}, bf16[32,384]{1,0:T(8,128)(2,1)S(1)}, f32[8,128]{1,0:T(8,128)S(1)}) custom-call(s32[1,1]{1,0:T(1,128)S(6)} %copy.15.count_ref, f32[32,320]{1,0:T(8,128)S(1)} %get-tuple-element.46.previous_ref.refs_4_, f32[8,128]{1,0:T(8,128)S(1)} %get-tuple-element.47.refs_0_.previous_exponent_ref.refs_1_, ...), custom_call_target="tpu_custom_call" | custom-call | tf_op jit(solution)/shard_map/middle/pallas_call | solution.py:515
  39.3 2.1 %collective-permute-start.8 = (bf16[32,384]{1,0:T(8,128)(2,1)S(1)}, bf16[32,384]{1,0:T(8,128)(2,1)S(1)}, u32[]{:S(2)}, u32[]{:S(2)}) collective-permute-start(bf16[32,384]{1,0:T(8,128)(2,1)S(1)} %get-tuple-element.56), channel_id=1, source_target_pairs={{0,24},{8,16},{16,8},{24,0},{1,25},{9,17},{17,9},{25,1},{2,26},{10... | collective-permute-start | bytes 73736 | tf_op jit(solution)/shard_map/ppermute | solution.py:47
  41.4 0.3 collective-permute-start.7
  41.8 3.3 %outer.5 = (bf16[5,16,4,16,2,128]{5,4,3,2,1,0:T(2,128)(2,1)}, f32[8,128]{1,0:T(8,128)S(1)}) custom-call(bf16[16,5,16,4,2,128]{5,4,3,2,1,0:T(2,128)(2,1)S(1)} %get-tuple-element.36.tiles_ref, bf16[5,16,2,128]{3,2,1,0:T(2,128)(2,1)S(1)} %collective-permute-done.edge_ref, ...), custom_call_target="tpu_custom_call", output_to_operand_aliasing={{0}: (5, {})} | custom-call | tf_op jit(solution)/shard_map/outer/pallas_call | solution.py:216
  45.0 0.0 collective-permute-done.8.refs_4_
  45.1 0.2 collective-permute-done.7.refs_3_
  45.3 0.4 gram.1
  45.7 9.4 %all_to_all.5.parts_ref = f32[32,1,128]{2,1,0:T(1,128)S(1)} all-to-all(f32[32,1,128]{2,1,0:T(1,128)S(1)} %gram.1), channel_id=1, replica_groups=mesh['gx'=4,'gy'=8] {'gx','gy'}, dimensions={0} | all-to-all | bytes 32768 | tf_op jit(solution)/shard_map/all_to_all | solution.py:536
  55.1 1.5 %finish.1 = f32[32,320]{1,0:T(8,128)} custom-call(f32[32,1,128]{2,1,0:T(1,128)S(1)} %all_to_all.5.parts_ref, f32[8,128]{1,0:T(8,128)S(1)} %get-tuple-element.40.refs_0_.previous_exponent_ref, f32[8,128]{1,0:T(8,128)S(1)} %get-tuple-element.47.refs_0_.previous_exponent_ref.refs_1_, f32[8,128]{1,0:T(8,128)S(1)} %get-tuple-element.51.refs_0_.refs_2_, ...), custom_call_target="tpu_custom_call" | custom-call | tf_op jit(solution)/shard_map/finish/pallas_call | solution.py:537
Async XLA Ops:
  2.9 22.7 %collective-permute-start.2 = (bf16[16,5,4,4,2,128]{5,4,3,2,1,0:T(2,128)(2,1)S(1)}, bf16[16,5,4,4,2,128]{5,4,3,2,1,0:T(2,128)(2,1)S(1)}, u32[]{:S(2)}, u32[]{:S(2)}) collective-permute-start(bf16[16,5,4,4,2,128]{5,4,3,2,1,0:T(2,128)(2,1)S(1)} %get-tuple-element.37), channel_id=1, source_target_pairs={{0,1},{1,2},{2,3},{3,4},{4,5},{5,6},{6,7},{7,0},{8,9},{9,10},{10,1... | collective-permute-start | bytes 1966088 | tf_op jit(solution)/shard_map/ppermute | solution.py:480
  4.4 6.6 %collective-permute-start = (bf16[5,16,2,128]{3,2,1,0:T(2,128)(2,1)S(1)}, bf16[5,16,2,128]{3,2,1,0:T(2,128)(2,1)S(1)}, u32[]{:S(2)}, u32[]{:S(2)}) collective-permute-start(bf16[5,16,2,128]{3,2,1,0:T(2,128)(2,1)S(1)} %get-tuple-element.32), channel_id=1, source_target_pairs={{0,8},{8,16},{16,24},{24,0},{1,9},{9,17},{17,25},{25,1},{2,10},{10... | collective-permute-start | bytes 122888 | tf_op jit(solution)/shard_map/ppermute | solution.py:449
  7.0 8.0 %collective-permute-start.1 = (bf16[5,4,4,2,128]{4,3,2,1,0:T(2,128)(2,1)S(1)}, bf16[5,4,4,2,128]{4,3,2,1,0:T(2,128)(2,1)S(1)}, u32[]{:S(2)}, u32[]{:S(2)}) collective-permute-start(bf16[5,4,4,2,128]{4,3,2,1,0:T(2,128)(2,1)S(1)} %get-tuple-element.33), channel_id=1, source_target_pairs={{0,1},{1,2},{2,3},{3,4},{4,5},{5,6},{6,7},{7,0},{8,9},{9,10},{10,1... | collective-permute-start | bytes 122888 | tf_op jit(solution)/shard_map/ppermute | solution.py:448
  21.3 6.9 %collective-permute-start.4 = (bf16[32,384]{1,0:T(8,128)(2,1)S(1)}, bf16[32,384]{1,0:T(8,128)(2,1)S(1)}, u32[]{:S(2)}, u32[]{:S(2)}) collective-permute-start(bf16[32,384]{1,0:T(8,128)(2,1)S(1)} %get-tuple-element.41), channel_id=1, source_target_pairs={{0,24},{8,16},{16,8},{24,0},{1,25},{9,17},{17,9},{25,1},{2,26},{10... | collective-permute-start | bytes 73736 | tf_op jit(solution)/shard_map/ppermute | solution.py:47
  25.7 3.8 %collective-permute-start.3 = (bf16[32,384]{1,0:T(8,128)(2,1)S(1)}, bf16[32,384]{1,0:T(8,128)(2,1)S(1)}, u32[]{:S(2)}, u32[]{:S(2)}) collective-permute-start(bf16[32,384]{1,0:T(8,128)(2,1)S(1)} %get-tuple-element.41), channel_id=1, source_target_pairs={{0,8},{8,0},{16,24},{24,16},{1,9},{9,1},{17,25},{25,17},{2,10},{10... | collective-permute-start | bytes 73736 | tf_op jit(solution)/shard_map/ppermute | solution.py:47
  31.4 5.7 %collective-permute-start.6 = (bf16[32,384]{1,0:T(8,128)(2,1)S(1)}, bf16[32,384]{1,0:T(8,128)(2,1)S(1)}, u32[]{:S(2)}, u32[]{:S(2)}) collective-permute-start(bf16[32,384]{1,0:T(8,128)(2,1)S(1)} %get-tuple-element.48), channel_id=1, source_target_pairs={{0,24},{8,16},{16,8},{24,0},{1,25},{9,17},{17,9},{25,1},{2,26},{10... | collective-permute-start | bytes 73736 | tf_op jit(solution)/shard_map/ppermute | solution.py:47
  33.6 3.8 %collective-permute-start.5 = (bf16[32,384]{1,0:T(8,128)(2,1)S(1)}, bf16[32,384]{1,0:T(8,128)(2,1)S(1)}, u32[]{:S(2)}, u32[]{:S(2)}) collective-permute-start(bf16[32,384]{1,0:T(8,128)(2,1)S(1)} %get-tuple-element.48), channel_id=1, source_target_pairs={{0,8},{8,0},{16,24},{24,16},{1,9},{9,1},{17,25},{25,17},{2,10},{10... | collective-permute-start | bytes 73736 | tf_op jit(solution)/shard_map/ppermute | solution.py:47
  39.3 5.7 %collective-permute-start.8 = (bf16[32,384]{1,0:T(8,128)(2,1)S(1)}, bf16[32,384]{1,0:T(8,128)(2,1)S(1)}, u32[]{:S(2)}, u32[]{:S(2)}) collective-permute-start(bf16[32,384]{1,0:T(8,128)(2,1)S(1)} %get-tuple-element.56), channel_id=1, source_target_pairs={{0,24},{8,16},{16,8},{24,0},{1,25},{9,17},{17,9},{25,1},{2,26},{10... | collective-permute-start | bytes 73736 | tf_op jit(solution)/shard_map/ppermute | solution.py:47
  41.4 3.9 %collective-permute-start.7 = (bf16[32,384]{1,0:T(8,128)(2,1)S(1)}, bf16[32,384]{1,0:T(8,128)(2,1)S(1)}, u32[]{:S(2)}, u32[]{:S(2)}) collective-permute-start(bf16[32,384]{1,0:T(8,128)(2,1)S(1)} %get-tuple-element.56), channel_id=1, source_target_pairs={{0,8},{8,0},{16,24},{24,16},{1,9},{9,1},{17,25},{25,17},{2,10},{10... | collective-permute-start | bytes 73736 | tf_op jit(solution)/shard_map/ppermute | solution.py:47

commit v3 on v2

--- a/solution.py
+++ b/solution.py
@@ -17,14 +17,12 @@
 advection = (1.0, 0.5, 0.25)
 
 LANES = 128
-GROUP = 8
-PRICE = 16 << 20
+GROUP = 16
 VMEM_BYTES = 24 << 20
 bf16 = jnp.bfloat16
 f32 = jnp.float32
 
 in_vmem = pl.BlockSpec(memory_space=pltpu.VMEM)
-in_smem = pl.BlockSpec(memory_space=pltpu.SMEM)
 in_hbm = pl.BlockSpec(memory_space=pltpu.HBM)
 params = pltpu.CompilerParams(vmem_limit_bytes=VMEM_BYTES)
 
@@ -41,10 +39,13 @@
 def neighbours(array, axis):
     count = lax.axis_size(axis)
     if count % 2 or count < 4:
-        return lax.ppermute(array, axis, ring(axis, 1)), lax.ppermute(array, axis, ring(axis, -1))
-    even = [(i, i ^ 1) for i in range(count)]
-    odd = [(i, (i + (1 if i % 2 else -1)) % count) for i in range(count)]
-    return lax.ppermute(array, axis, even), lax.ppermute(array, axis, odd)
+        first, second = ring(axis, 1), ring(axis, -1)
+    else:
+        first = [(i, i ^ 1) for i in range(count)]
+        second = [(i, (i + (1 if i % 2 else -1)) % count) for i in range(count)]
+    one = lax.ppermute(array, axis, first)
+    two = lax.ppermute(array, axis, second)
+    return one, two
 
 
 def jump_matrix(nodes, rows):
@@ -77,14 +78,12 @@
     return jnp.swapaxes(array, -3, -2).reshape(*lead, rows, tiles * lanes)
 
 
-def top_row(state_ref, t, k, target_ref, sem):
-    return pltpu.make_async_copy(state_ref.at[:, pl.ds(k * Q + Q - 1, 1), :, t], target_ref.at[:, pl.ds(k, 1)], sem)
-
-
 def faces_kernel(state_ref, edge_ref, corner_ref, sem):
     tiles = state_ref.shape[3]
-    copies = [top_row(state_ref, 0, k, corner_ref, sem.at[k]) for k in range(Q)]
-    copies.append(pltpu.make_async_copy(state_ref.at[:, :, Q - 1, tiles - 1], edge_ref, sem.at[Q]))
+    copies = [pltpu.make_async_copy(state_ref.at[:, :, Q - 1, tiles - 1], edge_ref, sem.at[0])]
+    for k in range(Q):
+        rows = state_ref.at[:, pl.ds(k * Q + Q - 1, 1)]
+        copies.append(pltpu.make_async_copy(rows.at[:, :, :, 0], corner_ref.at[:, pl.ds(k, 1)], sem.at[1 + k]))
     for copy in copies:
         copy.start()
     for copy in copies:
@@ -92,21 +91,22 @@
 
 
 def prep_kernel(
-    state_ref, rhs_ref, sigma_ref, deriv_ref, stiff_ref, expand_ref, jump_ref,
-    top_ref, tile_ref, rhs_out_ref, sigma_out_ref, full_ref, first_ref, block_ref,
-    deriv_in, stiff_in, expand_in, jump_in, sem,
+    state_ref, blocks_in_ref, rhs_ref, sigma_ref, deriv_ref, stiff_ref, expand_ref, jump_ref,
+    trace_ref, sigma_out_ref, full_ref, first_ref, block_ref, low_ref, high_ref, blocks_ref,
+    rhs_in, deriv_in, stiff_in, expand_in, jump_in, tile_ref, side_ref, stack_ref, speed_ref, copy_ref, sem,
 ):
-    count = top_ref.shape[0]
     pairs_of_refs = [
         (deriv_ref, deriv_in), (expand_ref, expand_in), (jump_ref, jump_in), (stiff_ref, stiff_in),
-        (state_ref.at[:, :, :, 0], tile_ref), (rhs_ref, rhs_out_ref), (sigma_ref, sigma_out_ref),
+        (state_ref.at[:, :, :, 0], tile_ref), (state_ref.at[:, :, Q - 1, 0], side_ref),
+        (rhs_ref, rhs_in), (sigma_ref, sigma_out_ref),
     ]
+    pairs_of_refs.append((blocks_in_ref.at[pl.ds(0, blocks_ref.shape[0])], blocks_ref))
+    half = low_ref.shape[3]
+    for k in range(Q):
+        rows_at = state_ref.at[:, pl.ds(k * Q + Q - 1, 1)]
+        pairs_of_refs.append((rows_at.at[:, :, :, pl.ds(0, half)], low_ref.at[:, pl.ds(k, 1)]))
+        pairs_of_refs.append((rows_at.at[:, :, :, pl.ds(half, half)], high_ref.at[:, pl.ds(k, 1)]))
     copies = [pltpu.make_async_copy(a, b, sem.at[at]) for at, (a, b) in enumerate(pairs_of_refs)]
-    copies += [
-        top_row(state_ref, t, k, top_ref.at[t], sem.at[len(pairs_of_refs) + t * Q + k])
-        for t in range(count)
-        for k in range(Q)
-    ]
     for copy in copies:
         copy.start()
     for copy in copies[:4]:
@@ -135,18 +135,40 @@
         at = slice(v * nodes, (v + 1) * nodes)
         block_ref[0, at, at] = high
         block_ref[1, at, at] = low
-    for copy in copies[4:]:
+    for copy in copies[4:8]:
         copy.wait()
-
-
-def fill_columns(stack_ref, speed_ref, own_at, last_at, edge_at, top_at, comps):
+    comps, faces, _, _, _ = tile_ref.shape
+    face = faces * rows
+    own_ref = tile_ref.reshape(comps, size, LANES)
+    last_ref = side_ref.reshape(comps, face, LANES)
+    nothing = jnp.zeros((face, LANES), bf16)
+    columns = fill_columns(
+        stack_ref, speed_ref, copy_ref,
+        lambda v: own_ref[v],
+        lambda v: last_ref[v],
+        lambda v: nothing,
+        lambda v: nothing,
+        comps,
+    )
+    slots = trace_ref.shape[0]
+    for v in columns:
+        value = jnp.dot(first_ref[...], stack_ref[...], preferred_element_type=f32)
+        at = slice(v * nodes, (v + 1) * nodes)
+        trace_ref[:, at] = rhs_in[:, at] + time_step * value.T[:slots]
+    for copy in copies[8:]:
+        copy.wait()
+
+
+def fill_columns(stack_ref, speed_ref, own_ref, own_at, last_at, edge_at, top_at, comps):
     size, width = speed_ref.shape[1:]
     face = size // Q
+    for v in range(comps):
+        own_ref[v] = own_at(v)
     for d in range(3):
-        speed_ref[d] = advection[d] + own_at(1 + d).astype(f32)
+        speed_ref[d] = advection[d] + own_ref[1 + d].astype(f32)
     lane = lax.broadcasted_iota(jnp.int32, (face, width), 1)
     for v in range(comps):
-        own = own_at(v)
+        own = own_ref[v]
         wide = own.astype(f32)
         for d in range(3):
             stack_ref[d * size : (d + 1) * size] = (wide * speed_ref[d]).astype(bf16)
@@ -159,20 +181,22 @@
         yield v
 
 
-def outer_piece(tiles, edge, top, full, after, result, start, stop, width):
-    count, comps, faces, _, rows, _ = tiles.shape
-    size = faces * Q * rows
+def outer_piece(tiles, sides, edge, top, full, after, result, start, stop, width):
+    count, comps, size, _ = tiles.shape
+    comps, faces, rows, _ = edge.shape
     face = faces * rows
     per_step = width // LANES
     held = (stop - start) * per_step
     shape = (comps, faces, Q, count, rows, LANES)
 
-    def kernel(tiles_ref, edge_ref, top_ref, full_ref, *refs):
-        out_ref, done_ref, stack_ref, speed_ref, held_ref, sem = refs[-6:]
+    def kernel(tiles_ref, sides_ref, edge_ref, top_ref, full_ref, *refs):
+        out_ref, done_ref, stack_ref, speed_ref, copy_ref, held_ref, sem = refs[-7:]
         done_ref[...] = jnp.zeros_like(done_ref)
-
-        def joined(read, height):
-            return jnp.concatenate([read(k).reshape(height, LANES) for k in range(per_step)], axis=1)
+        behind_ref = edge_ref.reshape(comps, face, LANES)
+        flat_ref = held_ref.reshape(held, comps, size, LANES)
+
+        def joined(read):
+            return jnp.concatenate([read(k) for k in range(per_step)], axis=1)
 
         def copy(i):
             return pltpu.make_async_copy(
@@ -182,22 +206,19 @@
         def step(n, carry):
             base = (start + n) * per_step
             columns = fill_columns(
-                stack_ref, speed_ref,
-                lambda v: joined(lambda k: tiles_ref[base + k, v], size),
-                lambda v: joined(lambda k: tiles_ref[base + k, v, :, Q - 1], face),
+                stack_ref, speed_ref, copy_ref,
+                lambda v: joined(lambda k: tiles_ref[base + k, v]),
+                lambda v: joined(lambda k: sides_ref[base + k, v]),
                 lambda v: jnp.where(
-                    base == 0,
-                    edge_ref[v].reshape(face, LANES).astype(f32),
-                    tiles_ref[jnp.maximum(base - 1, 0), v, :, Q - 1].reshape(face, LANES).astype(f32),
+                    base == 0, behind_ref[v].astype(f32), sides_ref[jnp.maximum(base - 1, 0), v].astype(f32)
                 ),
-                lambda v: joined(lambda k: top_ref[base + k, v], face),
+                lambda v: joined(lambda k: top_ref[v, :, :, n * per_step + k].reshape(face, LANES)),
                 comps,
             )
             for v in columns:
                 value = jnp.dot(full_ref[...], stack_ref[...], preferred_element_type=f32).astype(bf16)
                 for k in range(per_step):
-                    part = value[:, k * LANES : (k + 1) * LANES].reshape(faces, Q, rows, LANES)
-                    held_ref[n * per_step + k, v] = part
+                    flat_ref[n * per_step + k, v] = value[:, k * LANES : (k + 1) * LANES]
             for k in range(per_step):
                 copy(n * per_step + k).start()
             return carry
@@ -206,13 +227,13 @@
         for i in range(held):
             copy(i).wait()
 
-    operands = [tiles, edge, top, full, after]
-    specs = [in_vmem] * 5
+    operands = [tiles, sides, edge, top, full, after]
+    specs = [in_vmem] * len(operands)
     aliases = {}
     if result is not None:
         operands.append(held_in_hbm(result))
         specs.append(in_hbm)
-        aliases = {5: 0}
+        aliases = {len(specs) - 1: 0}
     return pl.pallas_call(
         kernel,
         in_specs=specs,
@@ -221,6 +242,7 @@
         scratch_shapes=[
             pltpu.VMEM((full.shape[1], width), bf16),
             pltpu.VMEM((3, size, width), f32),
+            pltpu.VMEM((comps, size, width), bf16),
             pltpu.VMEM((held, comps, faces, Q, rows, LANES), bf16),
             pltpu.SemaphoreType.DMA((held,)),
         ],
@@ -245,27 +267,31 @@
     return value * jnp.exp2(-by), by
 
 
-def group_count(count):
-    return (count + GROUP - 1) // GROUP
+def whole_count(count_ref):
+    return jnp.max(count_ref[...])
 
 
 def apply_blocks(count, value_ref, block_at, out_ref):
-    _, order = value_ref.shape
+    slots, order = value_ref.shape
     rows = lax.broadcasted_iota(jnp.int32, (2 * GROUP, order), 0)
-    out_ref[...] = jnp.zeros_like(out_ref)
-
-    def group(g, carry):
-        base = pl.multiple_of(g * GROUP, GROUP)
+
+    def group(g):
         block = block_at(g)
-        terms = jnp.concatenate(split(value_ref[pl.ds(base, GROUP), :]), axis=0)
+        here = slice(g * GROUP, (g + 1) * GROUP)
+        terms = jnp.concatenate(split(value_ref[here, :]), axis=0)
         kept = jnp.zeros((2 * GROUP, order), f32)
         for s in range(GROUP):
-            product = jnp.dot(terms, block(base + s), preferred_element_type=f32)
+            product = jnp.dot(terms, block(s), preferred_element_type=f32)
             kept = jnp.where((rows == s) | (rows == s + GROUP), product, kept)
-        out_ref[pl.ds(base, GROUP), :] = kept[:GROUP] + kept[GROUP:]
-        return carry
-
-    lax.fori_loop(0, group_count(count), group, 0)
+        out_ref[here, :] = kept[:GROUP] + kept[GROUP:]
+
+    group(0)
+    for g in range(1, slots // GROUP):
+        pl.when(g * GROUP < count)(lambda g=g: group(g))
+
+        @pl.when(g * GROUP >= count)
+        def _(g=g):
+            out_ref[g * GROUP : (g + 1) * GROUP, :] = jnp.zeros((GROUP, order), f32)
 
 
 def emit(direction_ref, exponent, sent_ref, exponent_ref):
@@ -279,56 +305,73 @@
     return (lax.broadcasted_iota(jnp.int32, shape, 0) < count).astype(f32)
 
 
+def turn_kernel(count_ref, near_ref, far_ref, state_ref, after_ref, turned_ref, tiles_ref, sides_ref, sem):
+    tiles = tiles_ref.shape[0]
+    copies = [pltpu.make_async_copy(state_ref.at[:, :, :, t], tiles_ref.at[t], sem.at[t]) for t in range(tiles)]
+    copies += [
+        pltpu.make_async_copy(state_ref.at[:, :, Q - 1, t], sides_ref.at[t], sem.at[tiles + t]) for t in range(tiles)
+    ]
+    for copy in copies:
+        copy.start()
+
+    def near(s, carry):
+        turned_ref[2 * s] = near_ref[2 * s].T
+        turned_ref[2 * s + 1] = near_ref[2 * s + 1].T
+        return carry
+
+    def far(s, carry):
+        turned_ref[GROUP + 2 * s] = far_ref[2 * s].T
+        turned_ref[GROUP + 2 * s + 1] = far_ref[2 * s + 1].T
+        return carry
+
+    lax.fori_loop(0, GROUP // 2, near, 0)
+
+    @pl.when(whole_count(count_ref) > GROUP)
+    def _():
+        lax.fori_loop(0, far_ref.shape[0] // 2, far, 0)
+
+    for copy in copies:
+        copy.wait()
+
+
 def start_kernel(
-    count_ref, state_ref, blocks_in_ref, tile_ref, edge_ref, corner_ref, first_ref, rhs_ref,
-    basis_ref, direction_ref, sent_ref, exponent_ref, tiles_ref, blocks_ref,
-    stack_ref, speed_ref, trace_ref, stage_ref, tile_sem, block_sem,
+    count_ref, blocks_in_ref, near_ref, edge_ref, corner_ref, first_ref, rhs_ref,
+    basis_ref, direction_ref, sent_ref, exponent_ref, far_ref,
+    stack_ref, trace_ref, block_sem,
 ):
     slots, order = rhs_ref.shape
-    tiles, comps, faces, _, rows, _ = tiles_ref.shape
-    count = count_ref[0, 0]
-
-    def tile_copy(t):
-        return pltpu.make_async_copy(state_ref.at[:, :, :, t], tiles_ref.at[t], tile_sem.at[t])
+    comps, faces, rows, _ = edge_ref.shape
+    count = whole_count(count_ref)
 
     def block_copy(g):
-        part = pl.ds(g * GROUP, GROUP)
-        return pltpu.make_async_copy(blocks_in_ref.at[part], stage_ref.at[part], block_sem.at[g])
+        source = blocks_in_ref.at[pl.ds(g * GROUP, GROUP)]
+        return pltpu.make_async_copy(source, far_ref.at[pl.ds((g - 1) * GROUP, GROUP)], block_sem.at[g])
 
     def arrived(g):
+        if g == 0:
+            return lambda s: near_ref[s].T
         block_copy(g).wait()
-
-        def block(at):
-            turned = stage_ref[at].T
-            blocks_ref[at] = turned
-            return turned
-
-        return block
-
-    for g in range(slots // GROUP):
-        pl.when(g < group_count(count))(block_copy(g).start)
-    for t in range(tiles):
-        tile_copy(t).start()
+        return lambda s: far_ref[(g - 1) * GROUP + s].T
+
+    for g in range(1, slots // GROUP):
+        pl.when(g * GROUP < count)(block_copy(g).start)
     nodes = order // comps
-    size, face = nodes * rows, faces * rows
-    columns = fill_columns(
-        stack_ref, speed_ref,
-        lambda v: tile_ref[v].reshape(size, LANES),
-        lambda v: tile_ref[v, :, Q - 1].reshape(face, LANES),
-        lambda v: edge_ref[v].reshape(face, LANES),
-        lambda v: corner_ref[v].reshape(face, LANES),
-        comps,
-    )
-    for v in columns:
-        value = jnp.dot(first_ref[...], stack_ref[...], preferred_element_type=f32)
+    face = faces * rows
+    behind_ref = edge_ref.reshape(comps, face, LANES)
+    below_ref = corner_ref.reshape(comps, face, LANES)
+    lane = lax.broadcasted_iota(jnp.int32, (face, LANES), 1)
+    weights = first_ref[:, first_ref.shape[1] - 2 * face :]
+    for v in range(comps):
+        edge = pltpu.roll(behind_ref[v].astype(f32), 1, 1)
+        stack_ref[:face] = jnp.where(lane == 0, edge, 0.0).astype(bf16)
+        stack_ref[face:] = below_ref[v]
+        value = jnp.dot(weights, stack_ref[...], preferred_element_type=f32)
         trace_ref[:, v * nodes : (v + 1) * nodes] = value.T[:slots]
     rhs = live_rows(count, rhs_ref.shape) * (rhs_ref[...] + time_step * trace_ref[...])
     basis, exponent = rescale(rhs)
     basis_ref[...] = basis
     apply_blocks(count, basis_ref, arrived, direction_ref)
     emit(direction_ref, exponent, sent_ref, exponent_ref)
-    for t in range(tiles):
-        tile_copy(t).wait()
 
 
 def operate(count_ref, direction_ref, exponent_ref, one_ref, two_ref, sigma_ref, stiff_ref):
@@ -345,7 +388,7 @@
     one = one_ref[:, :order].astype(f32) * jnp.exp2(exponent_one - common)
     two = two_ref[:, :order].astype(f32) * jnp.exp2(exponent_two - common)
     image = own * jnp.exp2(exponent - common) - coupling * (one + two)
-    basis, by = rescale(live_rows(count_ref[0, 0], image.shape) * image)
+    basis, by = rescale(live_rows(whole_count(count_ref), image.shape) * image)
     return basis, common + by
 
 
@@ -357,7 +400,7 @@
         count_ref, previous_ref, previous_exponent_ref, one_ref, two_ref, sigma_ref, stiff_ref
     )
     basis_ref[...] = basis
-    apply_blocks(count_ref[0, 0], basis_ref, lambda g: lambda at: blocks_ref[at], direction_ref)
+    apply_blocks(whole_count(count_ref), basis_ref, lambda g: lambda s: blocks_ref[g * GROUP + s], direction_ref)
     emit(direction_ref, exponent, sent_ref, exponent_ref)
 
 
@@ -442,7 +485,6 @@
         ],
         scratch_shapes=[pltpu.SemaphoreType.DMA((Q + 1,))],
         compiler_params=params,
-        cost_estimate=pl.CostEstimate(flops=0, transcendentals=0, bytes_accessed=PRICE),
         name="faces",
     )(state)
     came_corner = lax.ppermute(corner, "gy", ring("gy", 1))
@@ -453,68 +495,85 @@
     expand = np.repeat(np.eye(nodes, dtype=np.float32), rows, axis=0)
     jumps = np.concatenate([jumps, jumps[::rows]])
     operands = (
-        state, wall_rhs, wall_sigma, derivative, stiffness, jnp.asarray(expand, bf16),
+        state, wall_inverse, wall_rhs, wall_sigma, derivative, stiffness, jnp.asarray(expand, bf16),
         jnp.asarray(jumps, bf16),
     )
+    half_shape = jax.ShapeDtypeStruct((comps, Q, Q, count // 2, rows, LANES), bf16)
     operands = tuple(held_in_hbm(operand) for operand in operands)
-    top, tile, rhs, sigma, full, first, stiff = pl.pallas_call(
+    rhs, sigma, full, first, stiff, low, high, blocks = pl.pallas_call(
         prep_kernel,
         in_specs=[in_hbm] * len(operands),
-        out_specs=[in_vmem] * 7,
+        out_specs=[in_vmem] * 8,
         out_shape=[
-            jax.ShapeDtypeStruct((count, *corner.shape), bf16),
-            jax.ShapeDtypeStruct((comps, faces, Q, rows, LANES), bf16),
             jax.ShapeDtypeStruct(wall_rhs.shape, f32),
             jax.ShapeDtypeStruct(wall_sigma.shape, f32),
             jax.ShapeDtypeStruct((size, depth), bf16),
             jax.ShapeDtypeStruct((nodes, depth), bf16),
             jax.ShapeDtypeStruct((2, order, order), bf16),
+            half_shape,
+            half_shape,
+            jax.ShapeDtypeStruct((GROUP, order, order), bf16),
         ],
-        scratch_shapes=[pltpu.VMEM(a.shape, a.dtype) for a in (derivative, stiffness)]
+        scratch_shapes=[pltpu.VMEM(a.shape, a.dtype) for a in (wall_rhs, derivative, stiffness)]
         + [pltpu.VMEM(expand.shape, bf16), pltpu.VMEM(jumps.shape, bf16)]
-        + [pltpu.SemaphoreType.DMA((7 + count * Q,))],
+        + [pltpu.VMEM((comps, faces, Q, rows, LANES), bf16), pltpu.VMEM(edge.shape, bf16)]
+        + [pltpu.VMEM((depth, LANES), bf16), pltpu.VMEM((3, size, LANES), f32), pltpu.VMEM((comps, size, LANES), bf16)]
+        + [pltpu.SemaphoreType.DMA((9 + 2 * Q,))],
         compiler_params=params,
-        cost_estimate=pl.CostEstimate(flops=0, transcendentals=0, bytes_accessed=PRICE),
         name="prep",
     )(*operands)
-    came_top = lax.ppermute(top, "gy", ring("gy", 1))
 
     vector = jax.ShapeDtypeStruct((slots, order), f32)
     padded = -(-(order + 1) // LANES) * LANES
     step_shapes = [
         vector, vector, jax.ShapeDtypeStruct((slots, padded), bf16), jax.ShapeDtypeStruct((8, LANES), f32),
     ]
-    basis, direction, sent, exponent, tiles, blocks = pl.pallas_call(
+    basis, direction, sent, exponent, far = pl.pallas_call(
         start_kernel,
-        in_specs=[in_smem] + [in_hbm] * 2 + [in_vmem] * 5,
-        out_specs=[in_vmem] * 6,
-        out_shape=step_shapes + [
-            jax.ShapeDtypeStruct((count, comps, faces, Q, rows, LANES), bf16),
-            jax.ShapeDtypeStruct(wall_inverse.shape, bf16),
-        ],
+        in_specs=[in_vmem, in_hbm] + [in_vmem] * 5,
+        out_specs=[in_vmem] * 5,
+        out_shape=step_shapes + [jax.ShapeDtypeStruct((slots - GROUP, order, order), bf16)],
         scratch_shapes=[
-            pltpu.VMEM((depth, LANES), bf16), pltpu.VMEM((3, size, LANES), f32), pltpu.VMEM((slots, order), f32),
-            pltpu.VMEM(wall_inverse.shape, bf16),
-            pltpu.SemaphoreType.DMA((count,)), pltpu.SemaphoreType.DMA((slots // GROUP,)),
+            pltpu.VMEM((2 * faces * rows, LANES), bf16), pltpu.VMEM((slots, order), f32),
+            pltpu.SemaphoreType.DMA((slots // GROUP,)),
         ],
         compiler_params=params,
         name="start",
-    )(wall_count, state, held_in_hbm(wall_inverse), tile, came_edge, came_corner, first, rhs)
+    )(wall_count, held_in_hbm(wall_inverse), blocks, came_edge, came_corner, first, rhs)
     bases, directions, exponents = [basis], [direction], [exponent]
 
     width = 2 * LANES
     steps = cols // width
-    bounds = [steps * k // ITERS for k in range(ITERS + 1)]
-    residual = None
+    bounds = [steps * k // (ITERS - 1) for k in range(ITERS)]
+    residual, done = None, exponent
     for k in range(ITERS):
         one, two = neighbours(sent, "gx")
-        residual, done = outer_piece(
-            tiles, came_edge, came_top, full, exponent, residual, bounds[k], bounds[k + 1], width
-        )
+        if k == 0:
+            came_top = [lax.ppermute(low, "gy", ring("gy", 1))]
+            came_top.append(lax.ppermute(high, "gy", ring("gy", 1)))
+            blocks, tiles, sides = pl.pallas_call(
+                turn_kernel,
+                in_specs=[in_vmem] * 3 + [in_hbm, in_vmem],
+                out_specs=[in_vmem] * 3,
+                out_shape=[
+                    jax.ShapeDtypeStruct(wall_inverse.shape, bf16),
+                    jax.ShapeDtypeStruct((count, comps, faces, Q, rows, LANES), bf16),
+                    jax.ShapeDtypeStruct((count, *edge.shape), bf16),
+                ],
+                scratch_shapes=[pltpu.SemaphoreType.DMA((2 * count,))],
+                compiler_params=params,
+                name="turn",
+            )(wall_count, blocks, far, state, exponent)
+            tiles = tiles.reshape(count, comps, size, LANES)
+            sides = sides.reshape(count, comps, faces * rows, LANES)
+        else:
+            residual, done = outer_piece(
+                tiles, sides, came_edge, came_top[k - 1], full, exponent, residual, bounds[k - 1], bounds[k], width
+            )
         if k < ITERS - 1:
             basis, direction, sent, exponent = pl.pallas_call(
                 middle_kernel,
-                in_specs=[in_smem] + [in_vmem] * 8,
+                in_specs=[in_vmem] + [in_vmem] * 8,
                 out_specs=[in_vmem] * 4,
                 out_shape=step_shapes,
                 compiler_params=params,
@@ -527,7 +586,7 @@
     devices = lax.axis_size("gx") * lax.axis_size("gy")
     part = pl.pallas_call(
         gram_kernel,
-        in_specs=[in_smem] + [in_vmem] * (6 + 2 * ITERS),
+        in_specs=[in_vmem] + [in_vmem] * (6 + 2 * ITERS),
         out_specs=in_vmem,
         out_shape=jax.ShapeDtypeStruct((devices, 1, LANES), f32),
         compiler_params=params,

time: 56.8 us -> 54.8 us (0.965)
  waiting for transfers between devices: 8.24 us -> 6.99 us
  Pallas kernels: 24.1 us -> 23.1 us
    ppermute x7 -> x8, starting transfers between devices: 9.53 us -> 12.2 us  [the longest x3 5.7 us: neighbours(): two = lax.ppermute(array, axis, second)]
    pallas_call x3 -> x2, Pallas kernels: 8.98 us -> 6.87 us  [outer_piece(): pl.pallas_call(kernel, in_specs=specs, out_specs=[in_hbm, in_vmem], out_s...]
    ppermute x1, waiting for transfers between devices: 4.04 us -> 2.3 us  [solve(): came_corner = lax.ppermute(corner, 'gy', ring('gy', 1))]
    ppermute x1, waiting for transfers between devices: 2.05 us -> 3.57 us  [solve(): came_edge = lax.ppermute(edge, 'gx', ring('gx', 1))]
    ppermute x1, starting transfers between devices: 1.3 us -> 0.01 us  [solve(): came_corner = lax.ppermute(corner, 'gy', ring('gy', 1))]
    ppermute x7 -> x8, waiting for transfers between devices: 2.15 us -> 1.12 us  [the longest x3 1.11 us: neighbours(): two = lax.ppermute(array, axis, second)]
    ppermute x1, starting transfers between devices: 2.64 us -> 1.63 us  [solve(): came_edge = lax.ppermute(edge, 'gx', ring('gx', 1))]
    pallas_call x4 -> x5, Pallas kernels: 10.5 us -> 11.2 us  [the longest x1 3.73 us: solve(): pl.pallas_call(turn_kernel, in_specs=[in_vmem] * 3 + [in_hbm, in_vmem], o...]
  transfers between devices with their start and end apart: 9 -> 10, of which waited for: 6 -> 4; matrix products, arithmetic and copies ran while one was open for 0% -> 0% of each run, Pallas kernels for 28% -> 34%
where the time goes in v3:
time: 54.8 us; the launch traced here: 54.6 us
  Pallas kernels  23.1 us (42%)
  starting transfers between devices  13.8 us (25%)
  blocking collectives  9.3 us (17%)
  waiting for transfers between devices  6.99 us (13%)
  between operations  1.39 us (3%)
    all_to_all x1, blocking collectives, solve(): parts = lax.all_to_all(part, ('gx', 'gy'), 0, 0)  9.3 us
    pallas_call x2, Pallas kernels, outer_piece(): pl.pallas_call(kernel, in_specs=specs, out_specs=[in_hbm, in_vmem], out_s...  6.87 us
    ppermute x3, starting transfers between devices, neighbours(): two = lax.ppermute(array, axis, second)  5.7 us
    pallas_call x1, Pallas kernels, solve(): pl.pallas_call(turn_kernel, in_specs=[in_vmem] * 3 + [in_hbm, in_vmem], o...  3.73 us
    pallas_call x1, Pallas kernels, solve(): pl.pallas_call(start_kernel, in_specs=[in_vmem, in_hbm] + [in_vmem] * 5,...  3.58 us
    ppermute x1, waiting for transfers between devices, solve(): came_edge = lax.ppermute(edge, 'gx', ring('gx', 1))  3.57 us
    pallas_call x2, Pallas kernels, solve(): pl.pallas_call(middle_kernel, in_specs=[in_vmem] + [in_vmem] * 8, out_spe...  3.46 us
    ppermute x3, starting transfers between devices, neighbours(): one = lax.ppermute(array, axis, first)  3.35 us
  transfers between devices with their start and end apart: 10, of which 4 were waited for; matrix products, arithmetic and copies ran while one was open for 0% of the time, Pallas kernels for 34%

profile of v3, /device:TPU:0, one launch (start us, length us, event | category | flops | bytes accessed | tf_op | source)
XLA Modules:
  0.0 54.6 jit_solution(7256762669890449568)
XLA Ops:
  0.6 2.7 %prep.1 = (f32[32,320]{1,0:T(8,128)S(1)}, f32[32,320]{1,0:T(8,128)S(1)}, bf16[128,576]{1,0:T(8,128)(2,1)S(1)}, bf16[64,576]{1,0:T(8,128)(2,1)S(1)}, bf16[2,320,3...) custom-call(bf16[5,16,4,16,2,128]{5,4,3,2,1,0:T(2,128)(2,1)} %bitcas, ...), custom_call_target="tpu_custom_call" | custom-call | tf_op jit(solution)/shard_map/prep/pallas_call | solution.py:503
  3.3 0.5 collective-permute-start.7
  3.9 2.6 %collective-permute-start.2 = (bf16[5,4,4,8,2,128]{5,4,3,2,1,0:T(2,128)(2,1)S(1)}, bf16[5,4,4,8,2,128]{5,4,3,2,1,0:T(2,128)(2,1)S(1)}, u32[]{:S(2)}, u32[]{:S(2)}) collective-permute-start(bf16[5,4,4,8,2,128]{5,4,3,2,1,0:T(2,128)(2,1)S(1)} %get-tuple-element.41), channel_id=1, source_target_pairs={{0,1},{1,2},{2,3},{3,4},{4,5},{5,6},{6,7},{7,0},{8,9},{9,10},{10,1... | collective-permute-start | bytes 983048 | tf_op jit(solution)/shard_map/ppermute | solution.py:553
  6.5 0.8 %faces.1 = (bf16[5,16,2,128]{3,2,1,0:T(2,128)(2,1)S(1)}, bf16[5,4,4,2,128]{4,3,2,1,0:T(2,128)(2,1)S(1)}) custom-call(bf16[5,16,4,16,2,128]{5,4,3,2,1,0:T(2,128)(2,1)} %bitcast.13), custom_call_target="tpu_custom_call" | custom-call | tf_op jit(solution)/shard_map/faces/pallas_call | solution.py:478
  7.3 1.6 %collective-permute-start = (bf16[5,16,2,128]{3,2,1,0:T(2,128)(2,1)S(1)}, bf16[5,16,2,128]{3,2,1,0:T(2,128)(2,1)S(1)}, u32[]{:S(2)}, u32[]{:S(2)}) collective-permute-start(bf16[5,16,2,128]{3,2,1,0:T(2,128)(2,1)S(1)} %get-tuple-element.33), channel_id=1, source_target_pairs={{0,8},{8,16},{16,24},{24,0},{1,9},{9,17},{17,25},{25,1},{2,10},{10... | collective-permute-start | bytes 122888 | tf_op jit(solution)/shard_map/ppermute | solution.py:491
  8.9 0.0 collective-permute-start.1
  9.6 3.6 %collective-permute-done.edge_ref = bf16[5,16,2,128]{3,2,1,0:T(2,128)(2,1)S(1)} collective-permute-done((bf16[5,16,2,128]{3,2,1,0:T(2,128)(2,1)S(1)}, bf16[5,16,2,128]{3,2,1,0:T(2,128)(2,1)S(1)}, u32[]{:S(2)}, u32[]{:S(2)}) %collective-permute-start) | collective-permute-done | bytes 40992 | tf_op jit(solution)/shard_map/ppermute | solution.py:491
  13.2 2.3 %collective-permute-done.1.corner_ref = bf16[5,4,4,2,128]{4,3,2,1,0:T(2,128)(2,1)S(1)} collective-permute-done((bf16[5,4,4,2,128]{4,3,2,1,0:T(2,128)(2,1)S(1)}, bf16[5,4,4,2,128]{4,3,2,1,0:T(2,128)(2,1)S(1)}, u32[]{:S(2)}, u32[]{:S(2)}) %collective-permute-start.1) | collective-permute-done | bytes 40992 | tf_op jit(solution)/shard_map/ppermute | solution.py:490
  15.5 3.6 %start.1 = (f32[32,320]{1,0:T(8,128)S(1)}, f32[32,320]{1,0:T(8,128)S(1)}, bf16[32,384]{1,0:T(8,128)(2,1)S(1)}, f32[8,128]{1,0:T(8,128)S(1)}, bf16[16,320,320]{2,1,0:T(8,128)(2,1)S(1)}) custom-call(s32[1,1]{1,0:T(1,128)S(6)} %copy.13.count_ref, bf16[32,320,320]{2,1,0:T(8,128)(2,1)} %blocks_in_ref.3, bf16[16,320,320]{2,1,0:T(8,128)(2,1)S(1)} %get-tuple-element.32.near_ref, ...), custom_call_target="tpu_custom_call" | custom-call | tf_op jit(solution)/shard_map/start/pallas_call | solution.py:531
  19.0 2.4 %collective-permute-start.3 = (bf16[32,384]{1,0:T(8,128)(2,1)S(1)}, bf16[32,384]{1,0:T(8,128)(2,1)S(1)}, u32[]{:S(2)}, u32[]{:S(2)}) collective-permute-start(bf16[32,384]{1,0:T(8,128)(2,1)S(1)} %get-tuple-element.44), channel_id=1, source_target_pairs={{0,8},{8,0},{16,24},{24,16},{1,9},{9,1},{17,25},{25,17},{2,10},{10... | collective-permute-start | bytes 73736 | tf_op jit(solution)/shard_map/ppermute | solution.py:46
  21.4 2.5 %collective-permute-start.4 = (bf16[32,384]{1,0:T(8,128)(2,1)S(1)}, bf16[32,384]{1,0:T(8,128)(2,1)S(1)}, u32[]{:S(2)}, u32[]{:S(2)}) collective-permute-start(bf16[32,384]{1,0:T(8,128)(2,1)S(1)} %get-tuple-element.44), channel_id=1, source_target_pairs={{0,24},{8,16},{16,8},{24,0},{1,25},{9,17},{17,9},{25,1},{2,26},{10... | collective-permute-start | bytes 73736 | tf_op jit(solution)/shard_map/ppermute | solution.py:47
  23.9 3.7 %turn.1 = (bf16[32,320,320]{2,1,0:T(8,128)(2,1)S(1)}, bf16[16,5,16,4,2,128]{5,4,3,2,1,0:T(2,128)(2,1)S(1)}, bf16[16,5,16,2,128]{4,3,2,1,0:T(2,128)(2,1)S(1)}) custom-call(s32[1,1]{1,0:T(1,128)S(6)} %copy.13.count_ref, bf16[16,320,320]{2,1,0:T(8,128)(2,1)S(1)} %get-tuple-element.32.near_ref, bf16[16,320,320]{2,1,0:T(8,128)(2,1)S(1)} %get-tuple-element.37.far_ref, ...), custom_call_target="tpu_custom_call" | custom-call | tf_op jit(solution)/shard_map/turn/pallas_call | solution.py:554
  27.6 0.0 collective-permute-done.3.one_ref
  27.7 0.0 collective-permute-done.4.two_ref
  27.7 1.7 %middle.2 = (f32[32,320]{1,0:T(8,128)S(1)}, f32[32,320]{1,0:T(8,128)S(1)}, bf16[32,384]{1,0:T(8,128)(2,1)S(1)}, f32[8,128]{1,0:T(8,128)S(1)}) custom-call(s32[1,1]{1,0:T(1,128)S(6)} %copy.13.count_ref, f32[32,320]{1,0:T(8,128)S(1)} %get-tuple-element.43.previous_ref.refs_3_, f32[8,128]{1,0:T(8,128)S(1)} %get-tuple-element.38.after_ref.previous_exponent_ref._.refs_0_, ...), custom_call_target="tpu_custom_call" | custom-call | tf_op jit(solution)/shard_map/middle/pallas_call | solution.py:574
  29.4 0.7 %collective-permute-start.5 = (bf16[32,384]{1,0:T(8,128)(2,1)S(1)}, bf16[32,384]{1,0:T(8,128)(2,1)S(1)}, u32[]{:S(2)}, u32[]{:S(2)}) collective-permute-start(bf16[32,384]{1,0:T(8,128)(2,1)S(1)} %get-tuple-element.50), channel_id=1, source_target_pairs={{0,8},{8,0},{16,24},{24,16},{1,9},{9,1},{17,25},{25,17},{2,10},{10... | collective-permute-start | bytes 73736 | tf_op jit(solution)/shard_map/ppermute | solution.py:46
  30.2 1.3 %collective-permute-start.6 = (bf16[32,384]{1,0:T(8,128)(2,1)S(1)}, bf16[32,384]{1,0:T(8,128)(2,1)S(1)}, u32[]{:S(2)}, u32[]{:S(2)}) collective-permute-start(bf16[32,384]{1,0:T(8,128)(2,1)S(1)} %get-tuple-element.50), channel_id=1, source_target_pairs={{0,24},{8,16},{16,8},{24,0},{1,25},{9,17},{17,9},{25,1},{2,26},{10... | collective-permute-start | bytes 73736 | tf_op jit(solution)/shard_map/ppermute | solution.py:47
  31.4 0.0 collective-permute-done.7.top_ref
  31.4 3.4 %outer.2 = (bf16[5,16,4,16,2,128]{5,4,3,2,1,0:T(2,128)(2,1)}, f32[8,128]{1,0:T(8,128)S(1)}) custom-call(bf16[16,5,128,128]{3,2,1,0:T(8,128)(2,1)S(1)} %bitcast.8, bf16[16,5,32,128]{3,2,1,0:T(8,128)(2,1)S(1)} %bitcast.10, bf16[5,16,2,128]{3,2,1,0:T(2,128)(2,1)S(1)} %collective-permute-done.edge_ref, ...), custom_call_target="tpu_custom_call" | custom-call | tf_op jit(solution)/shard_map/outer/pallas_call | solution.py:237
  34.9 0.0 collective-permute-done.5.one_ref
  34.9 0.9 %collective-permute-done.6.two_ref = bf16[32,384]{1,0:T(8,128)(2,1)S(1)} collective-permute-done((bf16[32,384]{1,0:T(8,128)(2,1)S(1)}, bf16[32,384]{1,0:T(8,128)(2,1)S(1)}, u32[]{:S(2)}, u32[]{:S(2)}) %collective-permute-start.6) | collective-permute-done | bytes 24608 | tf_op jit(solution)/shard_map/ppermute | solution.py:47
  35.8 1.7 %middle.3 = (f32[32,320]{1,0:T(8,128)S(1)}, f32[32,320]{1,0:T(8,128)S(1)}, bf16[32,384]{1,0:T(8,128)(2,1)S(1)}, f32[8,128]{1,0:T(8,128)S(1)}) custom-call(s32[1,1]{1,0:T(1,128)S(6)} %copy.13.count_ref, f32[32,320]{1,0:T(8,128)S(1)} %get-tuple-element.48.previous_ref.refs_4_, f32[8,128]{1,0:T(8,128)S(1)} %get-tuple-element.49.refs_0_.previous_exponent_ref.refs_1_, ...), custom_call_target="tpu_custom_call" | custom-call | tf_op jit(solution)/shard_map/middle/pallas_call | solution.py:574
  37.5 0.2 collective-permute-start.8
  37.7 2.0 %collective-permute-start.9 = (bf16[32,384]{1,0:T(8,128)(2,1)S(1)}, bf16[32,384]{1,0:T(8,128)(2,1)S(1)}, u32[]{:S(2)}, u32[]{:S(2)}) collective-permute-start(bf16[32,384]{1,0:T(8,128)(2,1)S(1)} %get-tuple-element.58), channel_id=1, source_target_pairs={{0,24},{8,16},{16,8},{24,0},{1,25},{9,17},{17,9},{25,1},{2,26},{10... | collective-permute-start | bytes 73736 | tf_op jit(solution)/shard_map/ppermute | solution.py:47
  39.7 0.0 collective-permute-done.2.top_ref
  39.7 3.5 %outer.3 = (bf16[5,16,4,16,2,128]{5,4,3,2,1,0:T(2,128)(2,1)}, f32[8,128]{1,0:T(8,128)S(1)}) custom-call(bf16[16,5,128,128]{3,2,1,0:T(8,128)(2,1)S(1)} %bitcast.9, bf16[16,5,32,128]{3,2,1,0:T(8,128)(2,1)S(1)} %bitcast.11, bf16[5,16,2,128]{3,2,1,0:T(2,128)(2,1)S(1)} %collective-permute-done.edge_ref, ...), custom_call_target="tpu_custom_call", output_to_operand_aliasing={{0}: (6, {})} | custom-call | tf_op jit(solution)/shard_map/outer/pallas_call | solution.py:237
  43.1 0.0 collective-permute-done.8.refs_3_
  43.2 0.2 collective-permute-done.9.refs_4_
  43.4 0.4 gram.1
  43.8 9.3 %all_to_all.5.parts_ref = f32[32,1,128]{2,1,0:T(1,128)S(1)} all-to-all(f32[32,1,128]{2,1,0:T(1,128)S(1)} %gram.1), channel_id=1, replica_groups=mesh['gx'=4,'gy'=8] {'gx','gy'}, dimensions={0} | all-to-all | bytes 32768 | tf_op jit(solution)/shard_map/all_to_all | solution.py:595
  53.1 1.5 %finish.1 = f32[32,320]{1,0:T(8,128)} custom-call(f32[32,1,128]{2,1,0:T(1,128)S(1)} %all_to_all.5.parts_ref, f32[8,128]{1,0:T(8,128)S(1)} %get-tuple-element.38.after_ref.previous_exponent_ref._.refs_0_, f32[8,128]{1,0:T(8,128)S(1)} %get-tuple-element.49.refs_0_.previous_exponent_ref.refs_1_, f32[8,128]{1,0:T(8,128)S(1)} %get-tuple-element.53.refs_0_.refs_2_, ...), custom_call_target="tpu_custom_call" | custom-call | tf_op jit(solution)/shard_map/finish/pallas_call | solution.py:596
Async XLA Ops:
  3.3 28.1 %collective-permute-start.7 = (bf16[5,4,4,8,2,128]{5,4,3,2,1,0:T(2,128)(2,1)S(1)}, bf16[5,4,4,8,2,128]{5,4,3,2,1,0:T(2,128)(2,1)S(1)}, u32[]{:S(2)}, u32[]{:S(2)}) collective-permute-start(bf16[5,4,4,8,2,128]{5,4,3,2,1,0:T(2,128)(2,1)S(1)} %get-tuple-element.51), channel_id=1, source_target_pairs={{0,1},{1,2},{2,3},{3,4},{4,5},{5,6},{6,7},{7,0},{8,9},{9,10},{10,1... | collective-permute-start | bytes 983048 | tf_op jit(solution)/shard_map/ppermute | solution.py:552
  3.9 35.8 %collective-permute-start.2 = (bf16[5,4,4,8,2,128]{5,4,3,2,1,0:T(2,128)(2,1)S(1)}, bf16[5,4,4,8,2,128]{5,4,3,2,1,0:T(2,128)(2,1)S(1)}, u32[]{:S(2)}, u32[]{:S(2)}) collective-permute-start(bf16[5,4,4,8,2,128]{5,4,3,2,1,0:T(2,128)(2,1)S(1)} %get-tuple-element.41), channel_id=1, source_target_pairs={{0,1},{1,2},{2,3},{3,4},{4,5},{5,6},{6,7},{7,0},{8,9},{9,10},{10,1... | collective-permute-start | bytes 983048 | tf_op jit(solution)/shard_map/ppermute | solution.py:553
  7.3 5.9 %collective-permute-start = (bf16[5,16,2,128]{3,2,1,0:T(2,128)(2,1)S(1)}, bf16[5,16,2,128]{3,2,1,0:T(2,128)(2,1)S(1)}, u32[]{:S(2)}, u32[]{:S(2)}) collective-permute-start(bf16[5,16,2,128]{3,2,1,0:T(2,128)(2,1)S(1)} %get-tuple-element.33), channel_id=1, source_target_pairs={{0,8},{8,16},{16,24},{24,0},{1,9},{9,17},{17,25},{25,1},{2,10},{10... | collective-permute-start | bytes 122888 | tf_op jit(solution)/shard_map/ppermute | solution.py:491
  8.9 6.5 %collective-permute-start.1 = (bf16[5,4,4,2,128]{4,3,2,1,0:T(2,128)(2,1)S(1)}, bf16[5,4,4,2,128]{4,3,2,1,0:T(2,128)(2,1)S(1)}, u32[]{:S(2)}, u32[]{:S(2)}) collective-permute-start(bf16[5,4,4,2,128]{4,3,2,1,0:T(2,128)(2,1)S(1)} %get-tuple-element.34), channel_id=1, source_target_pairs={{0,1},{1,2},{2,3},{3,4},{4,5},{5,6},{6,7},{7,0},{8,9},{9,10},{10,1... | collective-permute-start | bytes 122888 | tf_op jit(solution)/shard_map/ppermute | solution.py:490
  19.0 8.6 %collective-permute-start.3 = (bf16[32,384]{1,0:T(8,128)(2,1)S(1)}, bf16[32,384]{1,0:T(8,128)(2,1)S(1)}, u32[]{:S(2)}, u32[]{:S(2)}) collective-permute-start(bf16[32,384]{1,0:T(8,128)(2,1)S(1)} %get-tuple-element.44), channel_id=1, source_target_pairs={{0,8},{8,0},{16,24},{24,16},{1,9},{9,1},{17,25},{25,17},{2,10},{10... | collective-permute-start | bytes 73736 | tf_op jit(solution)/shard_map/ppermute | solution.py:46
  21.4 6.2 %collective-permute-start.4 = (bf16[32,384]{1,0:T(8,128)(2,1)S(1)}, bf16[32,384]{1,0:T(8,128)(2,1)S(1)}, u32[]{:S(2)}, u32[]{:S(2)}) collective-permute-start(bf16[32,384]{1,0:T(8,128)(2,1)S(1)} %get-tuple-element.44), channel_id=1, source_target_pairs={{0,24},{8,16},{16,8},{24,0},{1,25},{9,17},{17,9},{25,1},{2,26},{10... | collective-permute-start | bytes 73736 | tf_op jit(solution)/shard_map/ppermute | solution.py:47
  29.4 5.4 %collective-permute-start.5 = (bf16[32,384]{1,0:T(8,128)(2,1)S(1)}, bf16[32,384]{1,0:T(8,128)(2,1)S(1)}, u32[]{:S(2)}, u32[]{:S(2)}) collective-permute-start(bf16[32,384]{1,0:T(8,128)(2,1)S(1)} %get-tuple-element.50), channel_id=1, source_target_pairs={{0,8},{8,0},{16,24},{24,16},{1,9},{9,1},{17,25},{25,17},{2,10},{10... | collective-permute-start | bytes 73736 | tf_op jit(solution)/shard_map/ppermute | solution.py:46
  30.2 5.6 %collective-permute-start.6 = (bf16[32,384]{1,0:T(8,128)(2,1)S(1)}, bf16[32,384]{1,0:T(8,128)(2,1)S(1)}, u32[]{:S(2)}, u32[]{:S(2)}) collective-permute-start(bf16[32,384]{1,0:T(8,128)(2,1)S(1)} %get-tuple-element.50), channel_id=1, source_target_pairs={{0,24},{8,16},{16,8},{24,0},{1,25},{9,17},{17,9},{25,1},{2,26},{10... | collective-permute-start | bytes 73736 | tf_op jit(solution)/shard_map/ppermute | solution.py:47
  37.5 5.6 %collective-permute-start.8 = (bf16[32,384]{1,0:T(8,128)(2,1)S(1)}, bf16[32,384]{1,0:T(8,128)(2,1)S(1)}, u32[]{:S(2)}, u32[]{:S(2)}) collective-permute-start(bf16[32,384]{1,0:T(8,128)(2,1)S(1)} %get-tuple-element.58), channel_id=1, source_target_pairs={{0,8},{8,0},{16,24},{24,16},{1,9},{9,1},{17,25},{25,17},{2,10},{10... | collective-permute-start | bytes 73736 | tf_op jit(solution)/shard_map/ppermute | solution.py:46
  37.7 5.6 %collective-permute-start.9 = (bf16[32,384]{1,0:T(8,128)(2,1)S(1)}, bf16[32,384]{1,0:T(8,128)(2,1)S(1)}, u32[]{:S(2)}, u32[]{:S(2)}) collective-permute-start(bf16[32,384]{1,0:T(8,128)(2,1)S(1)} %get-tuple-element.58), channel_id=1, source_target_pairs={{0,24},{8,16},{16,8},{24,0},{1,25},{9,17},{17,9},{25,1},{2,26},{10... | collective-permute-start | bytes 73736 | tf_op jit(solution)/shard_map/ppermute | solution.py:47

commit v4 on v3

--- a/solution.py
+++ b/solution.py
@@ -18,6 +18,7 @@
 
 LANES = 128
 GROUP = 16
+UNROLL = 8
 VMEM_BYTES = 24 << 20
 bf16 = jnp.bfloat16
 f32 = jnp.float32
@@ -271,27 +272,30 @@
     return jnp.max(count_ref[...])
 
 
-def apply_blocks(count, value_ref, block_at, out_ref):
+def in_groups(count, slots, group, clear):
+    group(0)
+    for g in range(1, slots // GROUP):
+        pl.when(g * GROUP < count)(lambda g=g: group(g))
+        pl.when(g * GROUP >= count)(lambda g=g: clear(g))
+
+
+def apply_blocks(count, value_ref, blocks_of, out_ref):
     slots, order = value_ref.shape
-    rows = lax.broadcasted_iota(jnp.int32, (2 * GROUP, order), 0)
+    rows = lax.broadcasted_iota(jnp.int32, (2 * GROUP, order), 0) % GROUP
 
     def group(g):
-        block = block_at(g)
+        block = blocks_of(g)
         here = slice(g * GROUP, (g + 1) * GROUP)
         terms = jnp.concatenate(split(value_ref[here, :]), axis=0)
         kept = jnp.zeros((2 * GROUP, order), f32)
         for s in range(GROUP):
-            product = jnp.dot(terms, block(s), preferred_element_type=f32)
-            kept = jnp.where((rows == s) | (rows == s + GROUP), product, kept)
+            kept = jnp.where(rows == s, jnp.dot(terms, block(s), preferred_element_type=f32), kept)
         out_ref[here, :] = kept[:GROUP] + kept[GROUP:]
 
-    group(0)
-    for g in range(1, slots // GROUP):
-        pl.when(g * GROUP < count)(lambda g=g: group(g))
-
-        @pl.when(g * GROUP >= count)
-        def _(g=g):
-            out_ref[g * GROUP : (g + 1) * GROUP, :] = jnp.zeros((GROUP, order), f32)
+    def clear(g):
+        out_ref[g * GROUP : (g + 1) * GROUP, :] = jnp.zeros((GROUP, order), f32)
+
+    in_groups(count, slots, group, clear)
 
 
 def emit(direction_ref, exponent, sent_ref, exponent_ref):
@@ -314,21 +318,22 @@
     for copy in copies:
         copy.start()
 
-    def near(s, carry):
-        turned_ref[2 * s] = near_ref[2 * s].T
-        turned_ref[2 * s + 1] = near_ref[2 * s + 1].T
-        return carry
-
-    def far(s, carry):
-        turned_ref[GROUP + 2 * s] = far_ref[2 * s].T
-        turned_ref[GROUP + 2 * s + 1] = far_ref[2 * s + 1].T
-        return carry
-
-    lax.fori_loop(0, GROUP // 2, near, 0)
+    def turn(source_ref, source, target, count):
+        def group(g, carry):
+            for s in range(UNROLL):
+                at = g * UNROLL + s
+                turned_ref[target + at] = source_ref[source + at].T
+            return carry
+
+        lax.fori_loop(0, count // UNROLL, group, 0)
+
+    near, far = near_ref.shape[0], far_ref.shape[0]
+    turn(near_ref, 0, 0, GROUP)
 
     @pl.when(whole_count(count_ref) > GROUP)
     def _():
-        lax.fori_loop(0, far_ref.shape[0] // 2, far, 0)
+        turn(near_ref, GROUP, GROUP, near - GROUP)
+        turn(far_ref, 0, near, far)
 
     for copy in copies:
         copy.wait()
@@ -337,24 +342,29 @@
 def start_kernel(
     count_ref, blocks_in_ref, near_ref, edge_ref, corner_ref, first_ref, rhs_ref,
     basis_ref, direction_ref, sent_ref, exponent_ref, far_ref,
-    stack_ref, trace_ref, block_sem,
+    stack_ref, trace_ref, turned_ref, far_sem,
 ):
     slots, order = rhs_ref.shape
     comps, faces, rows, _ = edge_ref.shape
     count = whole_count(count_ref)
 
-    def block_copy(g):
-        source = blocks_in_ref.at[pl.ds(g * GROUP, GROUP)]
-        return pltpu.make_async_copy(source, far_ref.at[pl.ds((g - 1) * GROUP, GROUP)], block_sem.at[g])
-
-    def arrived(g):
-        if g == 0:
-            return lambda s: near_ref[s].T
-        block_copy(g).wait()
-        return lambda s: far_ref[(g - 1) * GROUP + s].T
-
-    for g in range(1, slots // GROUP):
-        pl.when(g * GROUP < count)(block_copy(g).start)
+    near = near_ref.shape[0]
+    far_copy = pltpu.make_async_copy(blocks_in_ref.at[pl.ds(near, slots - near)], far_ref, far_sem)
+    pl.when(count > GROUP)(far_copy.start)
+
+    def blocks_of(g):
+        def block(s):
+            at = g * GROUP + s
+            if at == near:
+                far_copy.wait()
+            own = near_ref[at] if at < near else far_ref[at - near]
+            if s % 3 == 0:
+                return own.T
+            turned_ref[s] = own.T
+            return turned_ref[s]
+
+        return block
+
     nodes = order // comps
     face = faces * rows
     behind_ref = edge_ref.reshape(comps, face, LANES)
@@ -370,7 +380,7 @@
     rhs = live_rows(count, rhs_ref.shape) * (rhs_ref[...] + time_step * trace_ref[...])
     basis, exponent = rescale(rhs)
     basis_ref[...] = basis
-    apply_blocks(count, basis_ref, arrived, direction_ref)
+    apply_blocks(count, basis_ref, blocks_of, direction_ref)
     emit(direction_ref, exponent, sent_ref, exponent_ref)
 
 
@@ -400,7 +410,9 @@
         count_ref, previous_ref, previous_exponent_ref, one_ref, two_ref, sigma_ref, stiff_ref
     )
     basis_ref[...] = basis
-    apply_blocks(whole_count(count_ref), basis_ref, lambda g: lambda s: blocks_ref[g * GROUP + s], direction_ref)
+    apply_blocks(
+        whole_count(count_ref), basis_ref, lambda g: lambda s: blocks_ref[g * GROUP + s], direction_ref
+    )
     emit(direction_ref, exponent, sent_ref, exponent_ref)
 
 
@@ -498,6 +510,7 @@
         state, wall_inverse, wall_rhs, wall_sigma, derivative, stiffness, jnp.asarray(expand, bf16),
         jnp.asarray(jumps, bf16),
     )
+    near_slots = slots * 3 // 4
     half_shape = jax.ShapeDtypeStruct((comps, Q, Q, count // 2, rows, LANES), bf16)
     operands = tuple(held_in_hbm(operand) for operand in operands)
     rhs, sigma, full, first, stiff, low, high, blocks = pl.pallas_call(
@@ -512,7 +525,7 @@
             jax.ShapeDtypeStruct((2, order, order), bf16),
             half_shape,
             half_shape,
-            jax.ShapeDtypeStruct((GROUP, order, order), bf16),
+            jax.ShapeDtypeStruct((near_slots, order, order), bf16),
         ],
         scratch_shapes=[pltpu.VMEM(a.shape, a.dtype) for a in (wall_rhs, derivative, stiffness)]
         + [pltpu.VMEM(expand.shape, bf16), pltpu.VMEM(jumps.shape, bf16)]
@@ -532,10 +545,11 @@
         start_kernel,
         in_specs=[in_vmem, in_hbm] + [in_vmem] * 5,
         out_specs=[in_vmem] * 5,
-        out_shape=step_shapes + [jax.ShapeDtypeStruct((slots - GROUP, order, order), bf16)],
+        out_shape=step_shapes + [jax.ShapeDtypeStruct((slots - near_slots, order, order), bf16)],
         scratch_shapes=[
             pltpu.VMEM((2 * faces * rows, LANES), bf16), pltpu.VMEM((slots, order), f32),
-            pltpu.SemaphoreType.DMA((slots // GROUP,)),
+            pltpu.VMEM((GROUP, order, order), bf16),
+            pltpu.SemaphoreType.DMA(()),
         ],
         compiler_params=params,
         name="start",
@@ -573,7 +587,7 @@
         if k < ITERS - 1:
             basis, direction, sent, exponent = pl.pallas_call(
                 middle_kernel,
-                in_specs=[in_vmem] + [in_vmem] * 8,
+                in_specs=[in_vmem] * 9,
                 out_specs=[in_vmem] * 4,
                 out_shape=step_shapes,
                 compiler_params=params,

time: 54.8 us -> 54.2 us (0.989)
  Pallas kernels: 23.1 us -> 21.9 us
  starting transfers between devices: 13.8 us -> 14.7 us
    pallas_call x1, Pallas kernels: 3.73 us -> 2.86 us  [solve(): pl.pallas_call(turn_kernel, in_specs=[in_vmem] * 3 + [in_hbm, in_vmem], o...]
    pallas_call x1, Pallas kernels: 3.58 us -> 2.78 us  [solve(): pl.pallas_call(start_kernel, in_specs=[in_vmem, in_hbm] + [in_vmem] * 5,...]
    ppermute x3, starting transfers between devices: 3.35 us -> 3.92 us  [neighbours(): one = lax.ppermute(array, axis, first)]
  transfers between devices with their start and end apart: 10 -> 10, of which waited for: 4 -> 5; matrix products, arithmetic and copies ran while one was open for 0% -> 0% of each run, Pallas kernels for 34% -> 31%
where the time goes in v4:
time: 54.2 us; the launch traced here: 54 us
  Pallas kernels  21.9 us (40%)
  starting transfers between devices  14.7 us (27%)
  blocking collectives  9.04 us (17%)
  waiting for transfers between devices  6.97 us (13%)
  between operations  1.39 us (3%)
    all_to_all x1, blocking collectives, solve(): parts = lax.all_to_all(part, ('gx', 'gy'), 0, 0)  9.04 us
    pallas_call x2, Pallas kernels, outer_piece(): pl.pallas_call(kernel, in_specs=specs, out_specs=[in_hbm, in_vmem], out_s...  6.87 us
    ppermute x3, starting transfers between devices, neighbours(): two = lax.ppermute(array, axis, second)  6.01 us
    ppermute x3, starting transfers between devices, neighbours(): one = lax.ppermute(array, axis, first)  3.92 us
    ppermute x1, waiting for transfers between devices, solve(): came_edge = lax.ppermute(edge, 'gx', ring('gx', 1))  3.57 us
    pallas_call x2, Pallas kernels, solve(): pl.pallas_call(middle_kernel, in_specs=[in_vmem] * 9, out_specs=[in_vmem]...  3.44 us
    pallas_call x1, Pallas kernels, solve(): pl.pallas_call(prep_kernel, in_specs=[in_hbm] * len(operands), out_specs=...  3.2 us
    pallas_call x1, Pallas kernels, solve(): pl.pallas_call(turn_kernel, in_specs=[in_vmem] * 3 + [in_hbm, in_vmem], o...  2.86 us
  transfers between devices with their start and end apart: 10, of which 5 were waited for; matrix products, arithmetic and copies ran while one was open for 0% of the time, Pallas kernels for 31%

profile of v4, /device:TPU:0, one launch (start us, length us, event | category | flops | bytes accessed | tf_op | source)
XLA Modules:
  0.0 54.0 jit_solution(9347033423653551076)
XLA Ops:
  0.6 3.2 %prep.1 = (f32[32,320]{1,0:T(8,128)S(1)}, f32[32,320]{1,0:T(8,128)S(1)}, bf16[128,576]{1,0:T(8,128)(2,1)S(1)}, bf16[64,576]{1,0:T(8,128)(2,1)S(1)}, bf16[2,320,3...) custom-call(bf16[5,16,4,16,2,128]{5,4,3,2,1,0:T(2,128)(2,1)} %bitcas, ...), custom_call_target="tpu_custom_call" | custom-call | tf_op jit(solution)/shard_map/prep/pallas_call | solution.py:516
  3.8 0.5 %collective-permute-start.7 = (bf16[5,4,4,8,2,128]{5,4,3,2,1,0:T(2,128)(2,1)S(1)}, bf16[5,4,4,8,2,128]{5,4,3,2,1,0:T(2,128)(2,1)S(1)}, u32[]{:S(2)}, u32[]{:S(2)}) collective-permute-start(bf16[5,4,4,8,2,128]{5,4,3,2,1,0:T(2,128)(2,1)S(1)} %get-tuple-element.51), channel_id=1, source_target_pairs={{0,1},{1,2},{2,3},{3,4},{4,5},{5,6},{6,7},{7,0},{8,9},{9,10},{10,1... | collective-permute-start | bytes 983048 | tf_op jit(solution)/shard_map/ppermute | solution.py:566
  4.4 2.6 %collective-permute-start.2 = (bf16[5,4,4,8,2,128]{5,4,3,2,1,0:T(2,128)(2,1)S(1)}, bf16[5,4,4,8,2,128]{5,4,3,2,1,0:T(2,128)(2,1)S(1)}, u32[]{:S(2)}, u32[]{:S(2)}) collective-permute-start(bf16[5,4,4,8,2,128]{5,4,3,2,1,0:T(2,128)(2,1)S(1)} %get-tuple-element.41), channel_id=1, source_target_pairs={{0,1},{1,2},{2,3},{3,4},{4,5},{5,6},{6,7},{7,0},{8,9},{9,10},{10,1... | collective-permute-start | bytes 983048 | tf_op jit(solution)/shard_map/ppermute | solution.py:567
  7.0 0.8 %faces.1 = (bf16[5,16,2,128]{3,2,1,0:T(2,128)(2,1)S(1)}, bf16[5,4,4,2,128]{4,3,2,1,0:T(2,128)(2,1)S(1)}) custom-call(bf16[5,16,4,16,2,128]{5,4,3,2,1,0:T(2,128)(2,1)} %bitcast.13), custom_call_target="tpu_custom_call" | custom-call | tf_op jit(solution)/shard_map/faces/pallas_call | solution.py:490
  7.8 1.6 %collective-permute-start = (bf16[5,16,2,128]{3,2,1,0:T(2,128)(2,1)S(1)}, bf16[5,16,2,128]{3,2,1,0:T(2,128)(2,1)S(1)}, u32[]{:S(2)}, u32[]{:S(2)}) collective-permute-start(bf16[5,16,2,128]{3,2,1,0:T(2,128)(2,1)S(1)} %get-tuple-element.33), channel_id=1, source_target_pairs={{0,8},{8,16},{16,24},{24,0},{1,9},{9,17},{17,25},{25,1},{2,10},{10... | collective-permute-start | bytes 122888 | tf_op jit(solution)/shard_map/ppermute | solution.py:503
  9.4 0.0 collective-permute-start.1
  10.1 3.6 %collective-permute-done.edge_ref = bf16[5,16,2,128]{3,2,1,0:T(2,128)(2,1)S(1)} collective-permute-done((bf16[5,16,2,128]{3,2,1,0:T(2,128)(2,1)S(1)}, bf16[5,16,2,128]{3,2,1,0:T(2,128)(2,1)S(1)}, u32[]{:S(2)}, u32[]{:S(2)}) %collective-permute-start) | collective-permute-done | bytes 40992 | tf_op jit(solution)/shard_map/ppermute | solution.py:503
  13.7 2.3 %collective-permute-done.1.corner_ref = bf16[5,4,4,2,128]{4,3,2,1,0:T(2,128)(2,1)S(1)} collective-permute-done((bf16[5,4,4,2,128]{4,3,2,1,0:T(2,128)(2,1)S(1)}, bf16[5,4,4,2,128]{4,3,2,1,0:T(2,128)(2,1)S(1)}, u32[]{:S(2)}, u32[]{:S(2)}) %collective-permute-start.1) | collective-permute-done | bytes 40992 | tf_op jit(solution)/shard_map/ppermute | solution.py:502
  16.0 2.8 %start.1 = (f32[32,320]{1,0:T(8,128)S(1)}, f32[32,320]{1,0:T(8,128)S(1)}, bf16[32,384]{1,0:T(8,128)(2,1)S(1)}, f32[8,128]{1,0:T(8,128)S(1)}, bf16[8,320,320]{2,1,0:T(8,128)(2,1)S(1)}) custom-call(s32[1,1]{1,0:T(1,128)S(6)} %copy.13.count_ref, bf16[32,320,320]{2,1,0:T(8,128)(2,1)} %blocks_in_ref.3, bf16[24,320,320]{2,1,0:T(8,128)(2,1)S(1)} %get-tuple-element.32.near_ref, ...), custom_call_target="tpu_custom_call" | custom-call | tf_op jit(solution)/shard_map/start/pallas_call | solution.py:544
  18.8 2.4 %collective-permute-start.3 = (bf16[32,384]{1,0:T(8,128)(2,1)S(1)}, bf16[32,384]{1,0:T(8,128)(2,1)S(1)}, u32[]{:S(2)}, u32[]{:S(2)}) collective-permute-start(bf16[32,384]{1,0:T(8,128)(2,1)S(1)} %get-tuple-element.44), channel_id=1, source_target_pairs={{0,8},{8,0},{16,24},{24,16},{1,9},{9,1},{17,25},{25,17},{2,10},{10... | collective-permute-start | bytes 73736 | tf_op jit(solution)/shard_map/ppermute | solution.py:47
  21.1 2.5 %collective-permute-start.4 = (bf16[32,384]{1,0:T(8,128)(2,1)S(1)}, bf16[32,384]{1,0:T(8,128)(2,1)S(1)}, u32[]{:S(2)}, u32[]{:S(2)}) collective-permute-start(bf16[32,384]{1,0:T(8,128)(2,1)S(1)} %get-tuple-element.44), channel_id=1, source_target_pairs={{0,24},{8,16},{16,8},{24,0},{1,25},{9,17},{17,9},{25,1},{2,26},{10... | collective-permute-start | bytes 73736 | tf_op jit(solution)/shard_map/ppermute | solution.py:48
  23.6 2.9 %turn.1 = (bf16[32,320,320]{2,1,0:T(8,128)(2,1)S(1)}, bf16[16,5,16,4,2,128]{5,4,3,2,1,0:T(2,128)(2,1)S(1)}, bf16[16,5,16,2,128]{4,3,2,1,0:T(2,128)(2,1)S(1)}) custom-call(s32[1,1]{1,0:T(1,128)S(6)} %copy.13.count_ref, bf16[24,320,320]{2,1,0:T(8,128)(2,1)S(1)} %get-tuple-element.32.near_ref, bf16[8,320,320]{2,1,0:T(8,128)(2,1)S(1)} %get-tuple-element.37.far_ref, ...), custom_call_target="tpu_custom_call" | custom-call | tf_op jit(solution)/shard_map/turn/pallas_call | solution.py:568
  26.5 0.0 collective-permute-done.3.one_ref
  26.5 0.3 collective-permute-done.4.two_ref
  26.8 1.7 %middle.2 = (f32[32,320]{1,0:T(8,128)S(1)}, f32[32,320]{1,0:T(8,128)S(1)}, bf16[32,384]{1,0:T(8,128)(2,1)S(1)}, f32[8,128]{1,0:T(8,128)S(1)}) custom-call(s32[1,1]{1,0:T(1,128)S(6)} %copy.13.count_ref, f32[32,320]{1,0:T(8,128)S(1)} %get-tuple-element.43.previous_ref.refs_3_, f32[8,128]{1,0:T(8,128)S(1)} %get-tuple-element.38.after_ref.previous_exponent_ref._.refs_0_, ...), custom_call_target="tpu_custom_call" | custom-call | tf_op jit(solution)/shard_map/middle/pallas_call | solution.py:588
  28.5 0.5 collective-permute-start.5
  29.0 2.1 %collective-permute-start.6 = (bf16[32,384]{1,0:T(8,128)(2,1)S(1)}, bf16[32,384]{1,0:T(8,128)(2,1)S(1)}, u32[]{:S(2)}, u32[]{:S(2)}) collective-permute-start(bf16[32,384]{1,0:T(8,128)(2,1)S(1)} %get-tuple-element.50), channel_id=1, source_target_pairs={{0,24},{8,16},{16,8},{24,0},{1,25},{9,17},{17,9},{25,1},{2,26},{10... | collective-permute-start | bytes 73736 | tf_op jit(solution)/shard_map/ppermute | solution.py:48
  31.1 0.0 collective-permute-done.7.top_ref
  31.1 3.4 %outer.2 = (bf16[5,16,4,16,2,128]{5,4,3,2,1,0:T(2,128)(2,1)}, f32[8,128]{1,0:T(8,128)S(1)}) custom-call(bf16[16,5,128,128]{3,2,1,0:T(8,128)(2,1)S(1)} %bitcast.8, bf16[16,5,32,128]{3,2,1,0:T(8,128)(2,1)S(1)} %bitcast.10, bf16[5,16,2,128]{3,2,1,0:T(2,128)(2,1)S(1)} %collective-permute-done.edge_ref, ...), custom_call_target="tpu_custom_call" | custom-call | tf_op jit(solution)/shard_map/outer/pallas_call | solution.py:238
  34.6 0.0 collective-permute-done.5.one_ref
  34.6 0.1 collective-permute-done.6.two_ref
  34.6 1.7 %middle.3 = (f32[32,320]{1,0:T(8,128)S(1)}, f32[32,320]{1,0:T(8,128)S(1)}, bf16[32,384]{1,0:T(8,128)(2,1)S(1)}, f32[8,128]{1,0:T(8,128)S(1)}) custom-call(s32[1,1]{1,0:T(1,128)S(6)} %copy.13.count_ref, f32[32,320]{1,0:T(8,128)S(1)} %get-tuple-element.48.previous_ref.refs_4_, f32[8,128]{1,0:T(8,128)S(1)} %get-tuple-element.49.refs_0_.previous_exponent_ref.refs_1_, ...), custom_call_target="tpu_custom_call" | custom-call | tf_op jit(solution)/shard_map/middle/pallas_call | solution.py:588
  36.3 1.1 %collective-permute-start.8 = (bf16[32,384]{1,0:T(8,128)(2,1)S(1)}, bf16[32,384]{1,0:T(8,128)(2,1)S(1)}, u32[]{:S(2)}, u32[]{:S(2)}) collective-permute-start(bf16[32,384]{1,0:T(8,128)(2,1)S(1)} %get-tuple-element.58), channel_id=1, source_target_pairs={{0,8},{8,0},{16,24},{24,16},{1,9},{9,1},{17,25},{25,17},{2,10},{10... | collective-permute-start | bytes 73736 | tf_op jit(solution)/shard_map/ppermute | solution.py:47
  37.4 1.4 %collective-permute-start.9 = (bf16[32,384]{1,0:T(8,128)(2,1)S(1)}, bf16[32,384]{1,0:T(8,128)(2,1)S(1)}, u32[]{:S(2)}, u32[]{:S(2)}) collective-permute-start(bf16[32,384]{1,0:T(8,128)(2,1)S(1)} %get-tuple-element.58), channel_id=1, source_target_pairs={{0,24},{8,16},{16,8},{24,0},{1,25},{9,17},{17,9},{25,1},{2,26},{10... | collective-permute-start | bytes 73736 | tf_op jit(solution)/shard_map/ppermute | solution.py:48
  38.8 0.0 collective-permute-done.2.top_ref
  38.8 3.5 %outer.3 = (bf16[5,16,4,16,2,128]{5,4,3,2,1,0:T(2,128)(2,1)}, f32[8,128]{1,0:T(8,128)S(1)}) custom-call(bf16[16,5,128,128]{3,2,1,0:T(8,128)(2,1)S(1)} %bitcast.9, bf16[16,5,32,128]{3,2,1,0:T(8,128)(2,1)S(1)} %bitcast.11, bf16[5,16,2,128]{3,2,1,0:T(2,128)(2,1)S(1)} %collective-permute-done.edge_ref, ...), custom_call_target="tpu_custom_call", output_to_operand_aliasing={{0}: (6, {})} | custom-call | tf_op jit(solution)/shard_map/outer/pallas_call | solution.py:238
  42.3 0.0 collective-permute-done.8.refs_3_
  42.3 0.7 %collective-permute-done.9.refs_4_ = bf16[32,384]{1,0:T(8,128)(2,1)S(1)} collective-permute-done((bf16[32,384]{1,0:T(8,128)(2,1)S(1)}, bf16[32,384]{1,0:T(8,128)(2,1)S(1)}, u32[]{:S(2)}, u32[]{:S(2)}) %collective-permute-start.9) | collective-permute-done | bytes 24608 | tf_op jit(solution)/shard_map/ppermute | solution.py:48
  43.0 0.4 gram.1
  43.5 9.0 %all_to_all.5.parts_ref = f32[32,1,128]{2,1,0:T(1,128)S(1)} all-to-all(f32[32,1,128]{2,1,0:T(1,128)S(1)} %gram.1), channel_id=1, replica_groups=mesh['gx'=4,'gy'=8] {'gx','gy'}, dimensions={0} | all-to-all | bytes 32768 | tf_op jit(solution)/shard_map/all_to_all | solution.py:609
  52.5 1.5 %finish.1 = f32[32,320]{1,0:T(8,128)} custom-call(f32[32,1,128]{2,1,0:T(1,128)S(1)} %all_to_all.5.parts_ref, f32[8,128]{1,0:T(8,128)S(1)} %get-tuple-element.38.after_ref.previous_exponent_ref._.refs_0_, f32[8,128]{1,0:T(8,128)S(1)} %get-tuple-element.49.refs_0_.previous_exponent_ref.refs_1_, f32[8,128]{1,0:T(8,128)S(1)} %get-tuple-element.53.refs_0_.refs_2_, ...), custom_call_target="tpu_custom_call" | custom-call | tf_op jit(solution)/shard_map/finish/pallas_call | solution.py:610
Async XLA Ops:
  3.8 27.3 %collective-permute-start.7 = (bf16[5,4,4,8,2,128]{5,4,3,2,1,0:T(2,128)(2,1)S(1)}, bf16[5,4,4,8,2,128]{5,4,3,2,1,0:T(2,128)(2,1)S(1)}, u32[]{:S(2)}, u32[]{:S(2)}) collective-permute-start(bf16[5,4,4,8,2,128]{5,4,3,2,1,0:T(2,128)(2,1)S(1)} %get-tuple-element.51), channel_id=1, source_target_pairs={{0,1},{1,2},{2,3},{3,4},{4,5},{5,6},{6,7},{7,0},{8,9},{9,10},{10,1... | collective-permute-start | bytes 983048 | tf_op jit(solution)/shard_map/ppermute | solution.py:566
  4.4 34.4 %collective-permute-start.2 = (bf16[5,4,4,8,2,128]{5,4,3,2,1,0:T(2,128)(2,1)S(1)}, bf16[5,4,4,8,2,128]{5,4,3,2,1,0:T(2,128)(2,1)S(1)}, u32[]{:S(2)}, u32[]{:S(2)}) collective-permute-start(bf16[5,4,4,8,2,128]{5,4,3,2,1,0:T(2,128)(2,1)S(1)} %get-tuple-element.41), channel_id=1, source_target_pairs={{0,1},{1,2},{2,3},{3,4},{4,5},{5,6},{6,7},{7,0},{8,9},{9,10},{10,1... | collective-permute-start | bytes 983048 | tf_op jit(solution)/shard_map/ppermute | solution.py:567
  7.8 5.9 %collective-permute-start = (bf16[5,16,2,128]{3,2,1,0:T(2,128)(2,1)S(1)}, bf16[5,16,2,128]{3,2,1,0:T(2,128)(2,1)S(1)}, u32[]{:S(2)}, u32[]{:S(2)}) collective-permute-start(bf16[5,16,2,128]{3,2,1,0:T(2,128)(2,1)S(1)} %get-tuple-element.33), channel_id=1, source_target_pairs={{0,8},{8,16},{16,24},{24,0},{1,9},{9,17},{17,25},{25,1},{2,10},{10... | collective-permute-start | bytes 122888 | tf_op jit(solution)/shard_map/ppermute | solution.py:503
  9.4 6.5 %collective-permute-start.1 = (bf16[5,4,4,2,128]{4,3,2,1,0:T(2,128)(2,1)S(1)}, bf16[5,4,4,2,128]{4,3,2,1,0:T(2,128)(2,1)S(1)}, u32[]{:S(2)}, u32[]{:S(2)}) collective-permute-start(bf16[5,4,4,2,128]{4,3,2,1,0:T(2,128)(2,1)S(1)} %get-tuple-element.34), channel_id=1, source_target_pairs={{0,1},{1,2},{2,3},{3,4},{4,5},{5,6},{6,7},{7,0},{8,9},{9,10},{10,1... | collective-permute-start | bytes 122888 | tf_op jit(solution)/shard_map/ppermute | solution.py:502
  18.8 7.7 %collective-permute-start.3 = (bf16[32,384]{1,0:T(8,128)(2,1)S(1)}, bf16[32,384]{1,0:T(8,128)(2,1)S(1)}, u32[]{:S(2)}, u32[]{:S(2)}) collective-permute-start(bf16[32,384]{1,0:T(8,128)(2,1)S(1)} %get-tuple-element.44), channel_id=1, source_target_pairs={{0,8},{8,0},{16,24},{24,16},{1,9},{9,1},{17,25},{25,17},{2,10},{10... | collective-permute-start | bytes 73736 | tf_op jit(solution)/shard_map/ppermute | solution.py:47
  21.1 5.7 %collective-permute-start.4 = (bf16[32,384]{1,0:T(8,128)(2,1)S(1)}, bf16[32,384]{1,0:T(8,128)(2,1)S(1)}, u32[]{:S(2)}, u32[]{:S(2)}) collective-permute-start(bf16[32,384]{1,0:T(8,128)(2,1)S(1)} %get-tuple-element.44), channel_id=1, source_target_pairs={{0,24},{8,16},{16,8},{24,0},{1,25},{9,17},{17,9},{25,1},{2,26},{10... | collective-permute-start | bytes 73736 | tf_op jit(solution)/shard_map/ppermute | solution.py:48
  28.5 6.0 %collective-permute-start.5 = (bf16[32,384]{1,0:T(8,128)(2,1)S(1)}, bf16[32,384]{1,0:T(8,128)(2,1)S(1)}, u32[]{:S(2)}, u32[]{:S(2)}) collective-permute-start(bf16[32,384]{1,0:T(8,128)(2,1)S(1)} %get-tuple-element.50), channel_id=1, source_target_pairs={{0,8},{8,0},{16,24},{24,16},{1,9},{9,1},{17,25},{25,17},{2,10},{10... | collective-permute-start | bytes 73736 | tf_op jit(solution)/shard_map/ppermute | solution.py:47
  29.0 5.6 %collective-permute-start.6 = (bf16[32,384]{1,0:T(8,128)(2,1)S(1)}, bf16[32,384]{1,0:T(8,128)(2,1)S(1)}, u32[]{:S(2)}, u32[]{:S(2)}) collective-permute-start(bf16[32,384]{1,0:T(8,128)(2,1)S(1)} %get-tuple-element.50), channel_id=1, source_target_pairs={{0,24},{8,16},{16,8},{24,0},{1,25},{9,17},{17,9},{25,1},{2,26},{10... | collective-permute-start | bytes 73736 | tf_op jit(solution)/shard_map/ppermute | solution.py:48
  36.3 5.9 %collective-permute-start.8 = (bf16[32,384]{1,0:T(8,128)(2,1)S(1)}, bf16[32,384]{1,0:T(8,128)(2,1)S(1)}, u32[]{:S(2)}, u32[]{:S(2)}) collective-permute-start(bf16[32,384]{1,0:T(8,128)(2,1)S(1)} %get-tuple-element.58), channel_id=1, source_target_pairs={{0,8},{8,0},{16,24},{24,16},{1,9},{9,1},{17,25},{25,17},{2,10},{10... | collective-permute-start | bytes 73736 | tf_op jit(solution)/shard_map/ppermute | solution.py:47
  37.4 5.6 %collective-permute-start.9 = (bf16[32,384]{1,0:T(8,128)(2,1)S(1)}, bf16[32,384]{1,0:T(8,128)(2,1)S(1)}, u32[]{:S(2)}, u32[]{:S(2)}) collective-permute-start(bf16[32,384]{1,0:T(8,128)(2,1)S(1)} %get-tuple-element.58), channel_id=1, source_target_pairs={{0,24},{8,16},{16,8},{24,0},{1,25},{9,17},{17,9},{25,1},{2,26},{10... | collective-permute-start | bytes 73736 | tf_op jit(solution)/shard_map/ppermute | solution.py:48
